TPU v7x, 1024 devices: a whole 4x8x16 slice. The times are simulated.
1024 devices in a mesh: row: 64 (over z, x), col: 16 (over y, core).
Axes of the slice: x: 4, y: 8, z: 16, core: 2. Of those that a mesh axis runs over, the one named last changes fastest.
Arguments:
- activations: bfloat16 [2048, 12288], P('col', 'row'), may hold values from -6 to 6
- weight_tiles: bfloat16 [16, 64, 12, 4096], P('col', 'row'), may hold values from -0.125 to 0.125
- tile_ids: int32 [16, 64, 12], P('col', 'row'), may hold values from 0 to 71, as said below
- tile_counts: int32 [16, 64], P('col', 'row'), may hold values from 7 to 12, as said below
- upstream: bfloat16 [2048, 24576], P('col', 'row'), may hold values from -0.119628906 to 0.119628906
Outputs:
- output: bfloat16 [2048, 24576], P('col', 'row')
- weight_grad: bfloat16 [16, 64, 12, 4096], P('col', 'row')
Inputs may be any that keep to these rules, and one draw needn't show every extreme that they name: `tile_ids`: within one block the 12 slots name distinct tiles; only slots below the block's count are used. `tile_counts`: some block is full in every draw.
All inputs are finite; a program needn't handle non-finite values.
Results may differ from a plain program's by a relative error of at most 0.017.
Values may be sent and summed in bfloat16 or wider, within the bound.
No kernel may reach another device: no remote copies, remote signals or barrier semaphores. Data moves between devices by JAX's collectives and lax.ppermute only.
A program may use at most 32 MiB of HBM per device.

v0:
```python
import jax
import jax.numpy as jnp
from jax import lax
from jax.experimental import pallas as pl
from jax.experimental.pallas import tpu as pltpu
from jax.sharding import Mesh, PartitionSpec as P


TILE = 64
PAIR = 2 * TILE
CAP = 12
PAIRS = CAP // 2
PACK = PAIRS * TILE
META = 16
ROWS = PACK + META
PER_COL = 6
SUB = 3
F_LANE = 16
NZ, NX, NY = 16, 4, 8
SHARD = 192
COL_ROWS = NZ * SHARD
CUT = COL_ROWS // 2
X_ROWS = NX * COL_ROWS
FF_LOC = 384
TOK = 128


VMEM = pl.BlockSpec(memory_space=pltpu.VMEM)
ANY = pl.BlockSpec(memory_space=pl.ANY)
SMEM = pl.BlockSpec(memory_space=pltpu.SMEM)


def aligned(start, size):
    return pl.ds(pl.multiple_of(start, size), size)


def lanes_below():
    return lax.broadcasted_iota(jnp.int32, (1, PAIR), 1) < TILE


def two(ref, start0, start1):
    return jnp.concatenate([ref[aligned(start0 * TILE, TILE), :], ref[aligned(start1 * TILE, TILE), :]], axis=0)


def slot_grads(table, b, x, grad_t, dw, y):
    low = lanes_below()
    for m in range(PAIRS):
        s = 2 * m
        cols = two(grad_t, table[b, F_LANE + s], table[b, F_LANE + s + 1])
        rows = two(x, table[b, s], table[b, s + 1])
        prod = lax.dot_general(cols, rows, (((1,), (1,)), ((), ())), preferred_element_type=jnp.float32)
        dw[y, m * TILE : (m + 1) * TILE, :] = jnp.where(low, prod[:TILE], prod[TILE:]).astype(jnp.bfloat16)


def main_kernel(
    table, here, x0, x1a, x1b, x2a, x2b, x3a, x3b, w0, w1, up, out, grad_t, x, dw, acc, tiles0, tiles1, sem
):
    def part(distance, start, size):
        column = (here[0] + distance) & (NX - 1)
        return x.at[pl.ds(pl.multiple_of(column * COL_ROWS + start, CUT), size), :]

    moves = [
        (w0, tiles0),
        (w1, tiles1),
        (x0, part(0, 0, COL_ROWS)),
        (x1a, part(1, 0, CUT)),
        (x1b, part(1, CUT, CUT)),
        (x2a, part(2, 0, CUT)),
        (x2b, part(2, CUT, CUT)),
        (x3a, part(3, 0, CUT)),
        (x3b, part(3, CUT, CUT)),
    ]
    copies = [pltpu.make_async_copy(a, b, sem.at[i]) for i, (a, b) in enumerate(moves)]
    for c in copies:
        c.start()
    acc[...] = jnp.zeros_like(acc)
    for c in copies[2:]:
        c.wait()
    low = lanes_below()
    first = jnp.where(low, 1.0, 0.0).astype(jnp.bfloat16)
    second = jnp.where(low, 0.0, 1.0).astype(jnp.bfloat16)
    for rc, tiles in enumerate((tiles0, tiles1)):
        copies[rc].wait()

        def forward(y, carry, rc=rc, tiles=tiles):
            b = rc * NY + y
            for m in range(PAIRS):
                s = 2 * m
                tile = tiles[y, m * TILE : (m + 1) * TILE, :]
                prod = jnp.dot(
                    jnp.concatenate([tile * first, tile * second], axis=0),
                    two(x, table[b, s], table[b, s + 1]),
                    preferred_element_type=jnp.float32,
                )
                for p in range(2):
                    acc[aligned(table[b, F_LANE + s + p] * TILE, TILE), :] += prod[p * TILE : (p + 1) * TILE]
            return carry

        lax.fori_loop(0, NY, forward, 0)

    pre = acc[...].T
    cumul = 0.5 * (1.0 + lax.erf(pre * 0.7071067811865476))
    density = jnp.exp(-0.5 * pre * pre) * 0.3989422804014327
    out[...] = (pre * cumul).astype(jnp.bfloat16)
    grad_t[...] = (up[...].astype(jnp.float32) * (cumul + pre * density)).T.astype(jnp.bfloat16)

    def backward(y, carry):
        slot_grads(table, NY + y, x, grad_t, dw, y)
        return carry

    lax.fori_loop(0, NY, backward, 0)


def rest_kernel(table, x, grad_t, dw):
    def backward(y, carry):
        slot_grads(table, y, x, grad_t, dw, y)
        return carry

    lax.fori_loop(0, NY, backward, 0)


def params(mib):
    return pltpu.CompilerParams(vmem_limit_bytes=mib << 20)


def main_step(table, here, x0, x1a, x1b, x2a, x2b, x3a, x3b, w0, w1, up):
    return pl.pallas_call(
        main_kernel,
        out_shape=(
            jax.ShapeDtypeStruct((TOK, FF_LOC), jnp.bfloat16),
            jax.ShapeDtypeStruct((FF_LOC, TOK), jnp.bfloat16),
            jax.ShapeDtypeStruct((X_ROWS, TOK), jnp.bfloat16),
            jax.ShapeDtypeStruct((NY, PACK, PAIR), jnp.bfloat16),
        ),
        in_specs=[SMEM, SMEM] + [ANY] * 9 + [VMEM],
        out_specs=(VMEM, VMEM, VMEM, VMEM),
        scratch_shapes=[
            pltpu.VMEM((FF_LOC, TOK), jnp.float32),
            pltpu.VMEM((NY, ROWS, PAIR), jnp.bfloat16),
            pltpu.VMEM((NY, ROWS, PAIR), jnp.bfloat16),
            pltpu.SemaphoreType.DMA((9,)),
        ],
        compiler_params=params(16),
        cost_estimate=pl.CostEstimate(flops=2 * 10**9, bytes_accessed=8 * 10**6, transcendentals=10**5),
        name="main_step",
    )(table, here, x0, x1a, x1b, x2a, x2b, x3a, x3b, w0, w1, up)


def rest_step(table, x, grad_t):
    return pl.pallas_call(
        rest_kernel,
        out_shape=jax.ShapeDtypeStruct((NY, PACK, PAIR), jnp.bfloat16),
        in_specs=[SMEM, VMEM, VMEM],
        out_specs=VMEM,
        compiler_params=params(12),
        cost_estimate=pl.CostEstimate(flops=10**9, bytes_accessed=4 * 10**6, transcendentals=0),
        name="rest_step",
    )(table, x, grad_t)


def ring(n, step):
    return [(i, (i + step) % n) for i in range(n)]


SWAP = [(0, 1), (1, 0)]


def body(activations, weight_tiles, tile_ids, tile_counts, upstream):
    live = jnp.arange(CAP, dtype=jnp.int32) < tile_counts.reshape(())
    tiles = jnp.where(live[:, None, None], weight_tiles.reshape(CAP, TILE, TILE), 0)
    packed = tiles.reshape(PAIRS, 2, TILE, TILE).transpose(0, 3, 1, 2).reshape(PACK, PAIR)
    ids = tile_ids.reshape(1, CAP)
    block = 2 * lax.axis_index("y") + lax.axis_index("core")
    d = ids // PER_COL
    unit = d // SUB * (NZ * SUB) + block * SUB + d % SUB
    meta = jnp.pad(unit, ((0, META - 1), (0, PAIR - CAP))) + jnp.pad(
        ids % PER_COL, ((0, META - 1), (F_LANE, PAIR - F_LANE - CAP))
    )
    sent = jnp.concatenate([packed, meta.astype(jnp.bfloat16)], axis=0)
    wide = jnp.broadcast_to(sent[None], (NY, ROWS, PAIR))
    w_own = lax.all_to_all(wide, "y", split_axis=0, concat_axis=0, tiled=True)

    x_mine = activations.T.reshape(1, SHARD // 16, 16, TOK)
    x0 = lax.all_gather(x_mine, "z", axis=0, tiled=True).reshape(COL_ROWS, TOK)
    lower, upper = x0[:CUT], x0[CUT:]
    up_one, down_one = ring(NX, 1), ring(NX, -1)
    x3a = lax.ppermute(lower, "x", up_one)
    x1b = lax.ppermute(upper, "x", down_one)
    x3b = lax.ppermute(upper, "x", up_one)
    x1a = lax.ppermute(lower, "x", down_one)
    x2a = lax.ppermute(x3a, "x", up_one)
    x2b = lax.ppermute(x1b, "x", down_one)
    w_other = lax.ppermute(w_own, "core", SWAP)

    table = jnp.concatenate(
        [jnp.sum(w[:, PACK:, :].astype(jnp.float32), axis=1) for w in (w_own, w_other)], axis=0
    ).astype(jnp.int32)
    here = lax.axis_index("x").astype(jnp.int32).reshape(1)
    output, grad, x, theirs = main_step(table, here, x0, x1a, x1b, x2a, x2b, x3a, x3b, w_own, w_other, upstream)
    arrived = lax.ppermute(theirs, "core", SWAP)
    mine = rest_step(table, x, grad)
    both = (mine.astype(jnp.float32) + arrived.astype(jnp.float32)).astype(jnp.bfloat16)
    parts = lax.all_to_all(both, "y", split_axis=0, concat_axis=0, tiled=True)
    summed = jnp.sum(parts.astype(jnp.float32), axis=0)
    summed = summed.reshape(PAIRS, TILE, 2, TILE).transpose(0, 2, 3, 1).reshape(CAP, TILE * TILE)
    result = jnp.where(live[:, None], summed, 0.0).astype(jnp.bfloat16)
    return output, result.reshape(1, 1, CAP, TILE * TILE)


def solution(mesh):
    fine = Mesh(mesh.devices.reshape(NZ, NX, NY, 2), ("z", "x", "y", "core"))
    rows, cols = ("z", "x"), ("y", "core")
    return jax.shard_map(
        body,
        mesh=fine,
        in_specs=(
            P(cols, rows),
            P(cols, rows, None, None),
            P(cols, rows, None),
            P(cols, rows),
            P(cols, rows),
        ),
        out_specs=(P(cols, rows), P(cols, rows, None, None)),
        check_vma=False,
    )
```

profile of v0, /device:TPU:1, one launch (start us, length us, event | category | flops | bytes accessed | tf_op | source)
XLA Modules:
  0.0 157.0 jit_solution(17311024043029315768)
XLA Ops:
  1.3 1.1 reshape.226
  2.4 0.1 select_bitcast_fusion
  2.5 0.1 copy.11
  2.7 0.0 copy-start.1
  2.7 0.1 reshape.227
  2.8 0.7 fusion.1
  3.5 0.1 add_convert_fusion.1
  3.6 0.1 broadcast_in_dim.34
  3.7 22.8 %all_to_all.10.w0 = bf16[8,400,128]{2,1,0:T(8,128)(2,1)S(1)} all-to-all(bf16[8,400,128]{2,1,0:T(8,128)(2,1)S(1)} %broadcast_in_dim.34), channel_id=1, replica_groups=mesh['z'=16,'x'=4,'y'=8,'core'=2] {'y'}, dimensions={0} | all-to-all | bytes 1638400 | tf_op jit(solution)/shard_map/all_to_all | solution.py:181
  26.5 0.0 copy-start
  26.5 12.2 %collective-permute-start = (bf16[8,400,128]{2,1,0:T(8,128)(2,1)S(1)}, bf16[8,400,128]{2,1,0:T(8,128)(2,1)S(1)}, u32[]{:S(2)}, u32[]{:S(2)}) collective-permute-start(bf16[8,400,128]{2,1,0:T(8,128)(2,1)S(1)} %all_to_all.10.w0), channel_id=1, source_target_pairs={{0,1},{1,0},{2,3},{3,2},{4,5},{5,4},{6,7},{7,6},{8,9},{9,8},{10,11... | collective-permute-start | bytes 2457608 | tf_op jit(solution)/shard_map/ppermute | solution.py:193
  38.7 0.0 copy-done.1
  38.7 39.2 %all_gather.3 = bf16[16,12,16,128]{3,2,1,0:T(8,128)(2,1)S(1)} all-gather(bf16[1,12,16,128]{3,2,1,0:T(8,128)(2,1)S(1)} %bitcast.32), channel_id=1, replica_groups=mesh['z'=16,'x'=4,'y'=8,'core'=2] {'z'}, dimensions={0}, use_global_device_ids=true | all-gather | bytes 835584 | tf_op jit(solution)/shard_map/all_gather | solution.py:184
  77.9 1.0 fusion.2
  78.9 3.1 %collective-permute-start.3 = (bf16[1536,128]{1,0:T(8,128)(2,1)}, bf16[1536,128]{1,0:T(8,128)(2,1)S(1)}, u32[]{:S(2)}, u32[]{:S(2)}) collective-permute-start(bf16[1536,128]{1,0:T(8,128)(2,1)} %bitcast.9), channel_id=1, source_target_pairs={{0,16},{16,32},{32,48},{48,0},{1,17},{17,33},{33,49},{49,1},{2,18}... | collective-permute-start | bytes 1179656 | tf_op jit(solution)/shard_map/ppermute | solution.py:187
  82.0 3.4 %collective-permute-start.2 = (bf16[1536,128]{1,0:T(8,128)(2,1)}, bf16[1536,128]{1,0:T(8,128)(2,1)S(1)}, u32[]{:S(2)}, u32[]{:S(2)}) collective-permute-start(bf16[1536,128]{1,0:T(8,128)(2,1)} %bitcast.10), channel_id=1, source_target_pairs={{0,48},{16,0},{32,16},{48,32},{1,49},{17,1},{33,17},{49,33},{2,50}... | collective-permute-start | bytes 1179656 | tf_op jit(solution)/shard_map/ppermute | solution.py:188
  85.4 3.2 %collective-permute-start.1 = (bf16[1536,128]{1,0:T(8,128)(2,1)}, bf16[1536,128]{1,0:T(8,128)(2,1)}, u32[]{:S(2)}, u32[]{:S(2)}) collective-permute-start(bf16[1536,128]{1,0:T(8,128)(2,1)} %bitcast.9), channel_id=1, source_target_pairs={{0,48},{16,0},{32,16},{48,32},{1,49},{17,1},{33,17},{49,33},{2,50}... | collective-permute-start | bytes 1179656 | tf_op jit(solution)/shard_map/ppermute | solution.py:190
  88.6 2.1 %collective-permute-start.6 = (bf16[1536,128]{1,0:T(8,128)(2,1)}, bf16[1536,128]{1,0:T(8,128)(2,1)}, u32[]{:S(2)}, u32[]{:S(2)}) collective-permute-start(bf16[1536,128]{1,0:T(8,128)(2,1)} %bitcast.10), channel_id=1, source_target_pairs={{0,16},{16,32},{32,48},{48,0},{1,17},{17,33},{33,49},{49,1},{2,18}... | collective-permute-start | bytes 1179656 | tf_op jit(solution)/shard_map/ppermute | solution.py:189
  90.7 0.0 collective-permute-done.3.x3a
  90.7 1.9 %collective-permute-start.4 = (bf16[1536,128]{1,0:T(8,128)(2,1)S(1)}, bf16[1536,128]{1,0:T(8,128)(2,1)}, u32[]{:S(2)}, u32[]{:S(2)}) collective-permute-start(bf16[1536,128]{1,0:T(8,128)(2,1)S(1)} %collective-permute-done.3.x3a), channel_id=1, source_target_pairs={{0,16},{16,32},{32,48},{48,0},{1,17},{17,33},{33,49},{49,1},{2,18}... | collective-permute-start | bytes 1179656 | tf_op jit(solution)/shard_map/ppermute | solution.py:191
  92.7 0.0 collective-permute-done.2.x1b
  92.7 4.6 %collective-permute-start.5 = (bf16[1536,128]{1,0:T(8,128)(2,1)S(1)}, bf16[1536,128]{1,0:T(8,128)(2,1)}, u32[]{:S(2)}, u32[]{:S(2)}) collective-permute-start(bf16[1536,128]{1,0:T(8,128)(2,1)S(1)} %collective-permute-done.2.x1b), channel_id=1, source_target_pairs={{0,48},{16,0},{32,16},{48,32},{1,49},{17,1},{33,17},{49,33},{2,50}... | collective-permute-start | bytes 1179656 | tf_op jit(solution)/shard_map/ppermute | solution.py:192
  97.3 0.0 collective-permute-done.w1
  97.3 0.0 collective-permute-done.1.x1a
  97.3 3.2 %collective-permute-done.6.x3b = bf16[1536,128]{1,0:T(8,128)(2,1)} collective-permute-done((bf16[1536,128]{1,0:T(8,128)(2,1)}, bf16[1536,128]{1,0:T(8,128)(2,1)}, u32[]{:S(2)}, u32[]{:S(2)}) %collective-permute-start.6) | collective-permute-done | bytes 393248 | tf_op jit(solution)/shard_map/ppermute | solution.py:189
  100.6 6.6 %collective-permute-done.4.x2a = bf16[1536,128]{1,0:T(8,128)(2,1)} collective-permute-done((bf16[1536,128]{1,0:T(8,128)(2,1)S(1)}, bf16[1536,128]{1,0:T(8,128)(2,1)}, u32[]{:S(2)}, u32[]{:S(2)}) %collective-permute-start.4) | collective-permute-done | bytes 393248 | tf_op jit(solution)/shard_map/ppermute | solution.py:191
  107.2 0.0 collective-permute-done.5.x2b
  107.2 0.0 copy-done
  107.2 8.9 %main_step.1 = (bf16[128,384]{1,0:T(8,128)(2,1)}, bf16[384,128]{1,0:T(8,128)(2,1)S(1)}, bf16[12288,128]{1,0:T(8,128)(2,1)S(1)}, bf16[8,384,128]{2,1,0:T(8,128)(2,1)S(1)}) custom-call(s32[16,128]{1,0:T(8,128)S(1)} %maximum_convert_fusion.table, s32[1]{0:T(128)} %bitcast.5.here, bf16[3072,128]{1,0:T(8,128)(2,1)S(1)} %bitcast.30, ...), custom_call_target="tpu_custom_call" | custom-call | flops 2000000000 | bytes 8000000 | tf_op jit(solution)/shard_map/main_step/pallas_call | solution.py:127
  116.1 8.6 %collective-permute-start.7 = (bf16[8,384,128]{2,1,0:T(8,128)(2,1)S(1)}, bf16[8,384,128]{2,1,0:T(8,128)(2,1)S(1)}, u32[]{:S(2)}, u32[]{:S(2)}) collective-permute-start(bf16[8,384,128]{2,1,0:T(8,128)(2,1)S(1)} %get-tuple-element.9), channel_id=1, source_target_pairs={{0,1},{1,0},{2,3},{3,2},{4,5},{5,4},{6,7},{7,6},{8,9},{9,8},{10,11... | collective-permute-start | bytes 2359304 | tf_op jit(solution)/shard_map/ppermute | solution.py:200
  124.7 2.7 %rest_step.1 = bf16[8,384,128]{2,1,0:T(8,128)(2,1)S(1)} custom-call(s32[16,128]{1,0:T(8,128)S(1)} %maximum_convert_fusion.table, bf16[12288,128]{1,0:T(8,128)(2,1)S(1)} %get-tuple-element.7.x, bf16[384,128]{1,0:T(8,128)(2,1)S(1)} %get-tuple-element.8.grad_t), custom_call_target="tpu_custom_call" | custom-call | flops 1000000000 | bytes 4000000 | tf_op jit(solution)/shard_map/rest_step/pallas_call | solution.py:150
  127.4 0.0 collective-permute-done.7
  127.4 1.1 add_convert_fusion
  128.5 3.5 %all-to-all-start.1 = ((bf16[8,384,128]{2,1,0:T(8,128)(2,1)}), bf16[8,384,128]{2,1,0:T(8,128)(2,1)S(1)}, u32[]{:S(2)}, u32[]{:S(2)}) async-start(bf16[8,384,128]{2,1,0:T(8,128)(2,1)} %add_convert_fusion), calls=%async_computation.1 | async-start | bytes 1572864 | tf_op jit(solution)/shard_map/all_to_all | solution.py:203
  132.1 23.6 %all-to-all-done.1 = bf16[8,384,128]{2,1,0:T(8,128)(2,1)S(1)} async-done(((bf16[8,384,128]{2,1,0:T(8,128)(2,1)}), bf16[8,384,128]{2,1,0:T(8,128)(2,1)S(1)}, u32[]{:S(2)}, u32[]{:S(2)}) %all-to-all-start.1) | async-done | bytes 786464 | tf_op jit(solution)/shard_map/all_to_all | solution.py:203
  155.7 0.1 convert_reduce_fusion
  155.8 0.1 reshape.231
  155.9 0.2 copy.12
  156.1 0.2 reshape.232
  156.3 0.7 select_convert_fusion
  (6 shorter events, 0.1 us)
Async XLA Ops:
  2.7 36.0 %copy-start.1 = (bf16[128,192]{0,1:T(8,128)(2,1)S(1)}, bf16[128,192]{0,1:T(8,128)(2,1)}, u32[]{:S(2)}) copy-start(bf16[128,192]{0,1:T(8,128)(2,1)} %param.5) | copy-start | bytes 147460
  26.5 80.6 %copy-start = (bf16[128,384]{1,0:T(8,128)(2,1)S(1)}, bf16[128,384]{1,0:T(8,128)(2,1)}, u32[]{:S(2)}) copy-start(bf16[128,384]{1,0:T(8,128)(2,1)} %up.1) | copy-start | bytes 294916
  26.5 70.7 %collective-permute-start = (bf16[8,400,128]{2,1,0:T(8,128)(2,1)S(1)}, bf16[8,400,128]{2,1,0:T(8,128)(2,1)S(1)}, u32[]{:S(2)}, u32[]{:S(2)}) collective-permute-start(bf16[8,400,128]{2,1,0:T(8,128)(2,1)S(1)} %all_to_all.10.w0), channel_id=1, source_target_pairs={{0,1},{1,0},{2,3},{3,2},{4,5},{5,4},{6,7},{7,6},{8,9},{9,8},{10,11... | collective-permute-start | bytes 2457608 | tf_op jit(solution)/shard_map/ppermute | solution.py:193
  78.9 11.8 %collective-permute-start.3 = (bf16[1536,128]{1,0:T(8,128)(2,1)}, bf16[1536,128]{1,0:T(8,128)(2,1)S(1)}, u32[]{:S(2)}, u32[]{:S(2)}) collective-permute-start(bf16[1536,128]{1,0:T(8,128)(2,1)} %bitcast.9), channel_id=1, source_target_pairs={{0,16},{16,32},{32,48},{48,0},{1,17},{17,33},{33,49},{49,1},{2,18}... | collective-permute-start | bytes 1179656 | tf_op jit(solution)/shard_map/ppermute | solution.py:187
  82.0 10.6 %collective-permute-start.2 = (bf16[1536,128]{1,0:T(8,128)(2,1)}, bf16[1536,128]{1,0:T(8,128)(2,1)S(1)}, u32[]{:S(2)}, u32[]{:S(2)}) collective-permute-start(bf16[1536,128]{1,0:T(8,128)(2,1)} %bitcast.10), channel_id=1, source_target_pairs={{0,48},{16,0},{32,16},{48,32},{1,49},{17,1},{33,17},{49,33},{2,50}... | collective-permute-start | bytes 1179656 | tf_op jit(solution)/shard_map/ppermute | solution.py:188
  85.4 11.9 %collective-permute-start.1 = (bf16[1536,128]{1,0:T(8,128)(2,1)}, bf16[1536,128]{1,0:T(8,128)(2,1)}, u32[]{:S(2)}, u32[]{:S(2)}) collective-permute-start(bf16[1536,128]{1,0:T(8,128)(2,1)} %bitcast.9), channel_id=1, source_target_pairs={{0,48},{16,0},{32,16},{48,32},{1,49},{17,1},{33,17},{49,33},{2,50}... | collective-permute-start | bytes 1179656 | tf_op jit(solution)/shard_map/ppermute | solution.py:190
  88.6 12.0 %collective-permute-start.6 = (bf16[1536,128]{1,0:T(8,128)(2,1)}, bf16[1536,128]{1,0:T(8,128)(2,1)}, u32[]{:S(2)}, u32[]{:S(2)}) collective-permute-start(bf16[1536,128]{1,0:T(8,128)(2,1)} %bitcast.10), channel_id=1, source_target_pairs={{0,16},{16,32},{32,48},{48,0},{1,17},{17,33},{33,49},{49,1},{2,18}... | collective-permute-start | bytes 1179656 | tf_op jit(solution)/shard_map/ppermute | solution.py:189
  90.7 16.4 %collective-permute-start.4 = (bf16[1536,128]{1,0:T(8,128)(2,1)S(1)}, bf16[1536,128]{1,0:T(8,128)(2,1)}, u32[]{:S(2)}, u32[]{:S(2)}) collective-permute-start(bf16[1536,128]{1,0:T(8,128)(2,1)S(1)} %collective-permute-done.3.x3a), channel_id=1, source_target_pairs={{0,16},{16,32},{32,48},{48,0},{1,17},{17,33},{33,49},{49,1},{2,18}... | collective-permute-start | bytes 1179656 | tf_op jit(solution)/shard_map/ppermute | solution.py:191
  92.7 14.5 %collective-permute-start.5 = (bf16[1536,128]{1,0:T(8,128)(2,1)S(1)}, bf16[1536,128]{1,0:T(8,128)(2,1)}, u32[]{:S(2)}, u32[]{:S(2)}) collective-permute-start(bf16[1536,128]{1,0:T(8,128)(2,1)S(1)} %collective-permute-done.2.x1b), channel_id=1, source_target_pairs={{0,48},{16,0},{32,16},{48,32},{1,49},{17,1},{33,17},{49,33},{2,50}... | collective-permute-start | bytes 1179656 | tf_op jit(solution)/shard_map/ppermute | solution.py:192
  116.1 11.3 %collective-permute-start.7 = (bf16[8,384,128]{2,1,0:T(8,128)(2,1)S(1)}, bf16[8,384,128]{2,1,0:T(8,128)(2,1)S(1)}, u32[]{:S(2)}, u32[]{:S(2)}) collective-permute-start(bf16[8,384,128]{2,1,0:T(8,128)(2,1)S(1)} %get-tuple-element.9), channel_id=1, source_target_pairs={{0,1},{1,0},{2,3},{3,2},{4,5},{5,4},{6,7},{7,6},{8,9},{9,8},{10,11... | collective-permute-start | bytes 2359304 | tf_op jit(solution)/shard_map/ppermute | solution.py:200
  128.5 27.1 %all-to-all-start.1 = ((bf16[8,384,128]{2,1,0:T(8,128)(2,1)}), bf16[8,384,128]{2,1,0:T(8,128)(2,1)S(1)}, u32[]{:S(2)}, u32[]{:S(2)}) async-start(bf16[8,384,128]{2,1,0:T(8,128)(2,1)} %add_convert_fusion), calls=%async_computation.1 | async-start | bytes 1572864 | tf_op jit(solution)/shard_map/all_to_all | solution.py:203
where the time goes:
time: 158 us; the launch traced here: 157 us
  blocking collectives  62 us (39%)
  starting transfers between devices  42.6 us (27%)
  waiting for transfers between devices  33.4 us (21%)
  Pallas kernels  11.6 us (7%)
  local copies, waits for them, and re-layouts  3.02 us (2%)
  other arithmetic  2.86 us (2%)
    all_gather x1, blocking collectives, body(): x0 = lax.all_gather(x_mine, 'z', axis=0, tiled=True).reshape(COL_ROWS, TOK)  39.2 us
    all_to_all x1, waiting for transfers between devices, body(): parts = lax.all_to_all(both, 'y', split_axis=0, concat_axis=0, tiled=True)  23.6 us
    all_to_all x1, blocking collectives, body(): w_own = lax.all_to_all(wide, 'y', split_axis=0, concat_axis=0, tiled=True)  22.8 us
    ppermute x1, starting transfers between devices, body(): w_other = lax.ppermute(w_own, 'core', SWAP)  12.2 us
    pallas_call x1, Pallas kernels, main_step(): pl.pallas_call(main_kernel, out_shape=(jax.ShapeDtypeStruct((TOK, FF_LOC)...  8.91 us
    ppermute x1, starting transfers between devices, body(): arrived = lax.ppermute(theirs, 'core', SWAP)  8.63 us
    ppermute x1, waiting for transfers between devices, body(): x2a = lax.ppermute(x3a, 'x', up_one)  6.61 us
    ppermute x1, starting transfers between devices, body(): x2b = lax.ppermute(x1b, 'x', down_one)  4.57 us
  transfers between devices with their start and end apart: 9, of which 3 were waited for; matrix products, arithmetic and copies ran while one was open for 1% of the time, Pallas kernels for 2%

commit v1 on v0

--- a/solution.py
+++ b/solution.py
@@ -56,7 +56,7 @@
     table, here, x0, x1a, x1b, x2a, x2b, x3a, x3b, w0, w1, up, out, grad_t, x, dw, acc, tiles0, tiles1, sem
 ):
     def part(distance, start, size):
-        column = (here[0] + distance) & (NX - 1)
+        column = here[0] ^ distance
         return x.at[pl.ds(pl.multiple_of(column * COL_ROWS + start, CUT), size), :]
 
     moves = [
@@ -96,7 +96,7 @@
                     acc[aligned(table[b, F_LANE + s + p] * TILE, TILE), :] += prod[p * TILE : (p + 1) * TILE]
             return carry
 
-        lax.fori_loop(0, NY, forward, 0)
+        lax.fori_loop(0, NY, forward, 0, unroll=2)
 
     pre = acc[...].T
     cumul = 0.5 * (1.0 + lax.erf(pre * 0.7071067811865476))
@@ -108,7 +108,7 @@
         slot_grads(table, NY + y, x, grad_t, dw, y)
         return carry
 
-    lax.fori_loop(0, NY, backward, 0)
+    lax.fori_loop(0, NY, backward, 0, unroll=2)
 
 
 def rest_kernel(table, x, grad_t, dw):
@@ -116,7 +116,7 @@
         slot_grads(table, y, x, grad_t, dw, y)
         return carry
 
-    lax.fori_loop(0, NY, backward, 0)
+    lax.fori_loop(0, NY, backward, 0, unroll=2)
 
 
 def params(mib):
@@ -158,8 +158,8 @@
     )(table, x, grad_t)
 
 
-def ring(n, step):
-    return [(i, (i + step) % n) for i in range(n)]
+def trade(mask):
+    return [(i, i ^ mask) for i in range(NX)]
 
 
 SWAP = [(0, 1), (1, 0)]
@@ -183,13 +183,13 @@
     x_mine = activations.T.reshape(1, SHARD // 16, 16, TOK)
     x0 = lax.all_gather(x_mine, "z", axis=0, tiled=True).reshape(COL_ROWS, TOK)
     lower, upper = x0[:CUT], x0[CUT:]
-    up_one, down_one = ring(NX, 1), ring(NX, -1)
-    x3a = lax.ppermute(lower, "x", up_one)
-    x1b = lax.ppermute(upper, "x", down_one)
-    x3b = lax.ppermute(upper, "x", up_one)
-    x1a = lax.ppermute(lower, "x", down_one)
-    x2a = lax.ppermute(x3a, "x", up_one)
-    x2b = lax.ppermute(x1b, "x", down_one)
+    near, far = trade(1), trade(3)
+    x1a = lax.ppermute(lower, "x", near)
+    x3b = lax.ppermute(upper, "x", far)
+    x1b = lax.ppermute(upper, "x", near)
+    x3a = lax.ppermute(lower, "x", far)
+    x2a = lax.ppermute(x1a, "x", far)
+    x2b = lax.ppermute(x3b, "x", near)
     w_other = lax.ppermute(w_own, "core", SWAP)
 
     table = jnp.concatenate(

time: 158 us -> 156 us (0.987)
  Pallas kernels: 11.6 us -> 9.52 us
    pallas_call x1, Pallas kernels: 8.91 us -> 7.28 us  [main_step(): pl.pallas_call(main_kernel, out_shape=(jax.ShapeDtypeStruct((TOK, FF_LOC)...]
  transfers between devices with their start and end apart: 9 -> 9, of which waited for: 3 -> 5; matrix products, arithmetic and copies ran while one was open for 1% -> 1% of each run, Pallas kernels for 2% -> 1%
where the time goes in v1:
time: 156 us; the launch traced here: 155 us
  blocking collectives  62 us (40%)
  starting transfers between devices  43.5 us (28%)
  waiting for transfers between devices  32.9 us (21%)
  Pallas kernels  9.52 us (6%)
  local copies, waits for them, and re-layouts  3.02 us (2%)
  other arithmetic  2.86 us (2%)
    all_gather x1, blocking collectives, body(): x0 = lax.all_gather(x_mine, 'z', axis=0, tiled=True).reshape(COL_ROWS, TOK)  39.2 us
    all_to_all x1, waiting for transfers between devices, body(): parts = lax.all_to_all(both, 'y', split_axis=0, concat_axis=0, tiled=True)  23.6 us
    all_to_all x1, blocking collectives, body(): w_own = lax.all_to_all(wide, 'y', split_axis=0, concat_axis=0, tiled=True)  22.8 us
    ppermute x1, starting transfers between devices, body(): w_other = lax.ppermute(w_own, 'core', SWAP)  12.2 us
    ppermute x1, starting transfers between devices, body(): arrived = lax.ppermute(theirs, 'core', SWAP)  9.82 us
    pallas_call x1, Pallas kernels, main_step(): pl.pallas_call(main_kernel, out_shape=(jax.ShapeDtypeStruct((TOK, FF_LOC)...  7.28 us
    ppermute x1, waiting for transfers between devices, body(): x2a = lax.ppermute(x1a, 'x', far)  6.24 us
    ppermute x1, starting transfers between devices, body(): x2a = lax.ppermute(x1a, 'x', far)  3.73 us
  transfers between devices with their start and end apart: 9, of which 5 were waited for; matrix products, arithmetic and copies ran while one was open for 1% of the time, Pallas kernels for 1%

profile of v1, /device:TPU:1, one launch (start us, length us, event | category | flops | bytes accessed | tf_op | source)
XLA Modules:
  0.0 155.4 jit_solution(11532444387568461787)
XLA Ops:
  1.3 1.1 reshape.226
  2.4 0.1 select_bitcast_fusion
  2.5 0.1 copy.11
  2.7 0.0 copy-start.1
  2.7 0.1 reshape.227
  2.8 0.7 fusion.1
  3.5 0.1 add_convert_fusion.1
  3.6 0.1 broadcast_in_dim.34
  3.7 22.8 %all_to_all.10.w0 = bf16[8,400,128]{2,1,0:T(8,128)(2,1)S(1)} all-to-all(bf16[8,400,128]{2,1,0:T(8,128)(2,1)S(1)} %broadcast_in_dim.34), channel_id=1, replica_groups=mesh['z'=16,'x'=4,'y'=8,'core'=2] {'y'}, dimensions={0} | all-to-all | bytes 1638400 | tf_op jit(solution)/shard_map/all_to_all | solution.py:181
  26.5 0.0 copy-start
  26.5 12.2 %collective-permute-start = (bf16[8,400,128]{2,1,0:T(8,128)(2,1)S(1)}, bf16[8,400,128]{2,1,0:T(8,128)(2,1)S(1)}, u32[]{:S(2)}, u32[]{:S(2)}) collective-permute-start(bf16[8,400,128]{2,1,0:T(8,128)(2,1)S(1)} %all_to_all.10.w0), channel_id=1, source_target_pairs={{0,1},{1,0},{2,3},{3,2},{4,5},{5,4},{6,7},{7,6},{8,9},{9,8},{10,11... | collective-permute-start | bytes 2457608 | tf_op jit(solution)/shard_map/ppermute | solution.py:193
  38.7 0.0 copy-done.1
  38.7 39.2 %all_gather.3 = bf16[16,12,16,128]{3,2,1,0:T(8,128)(2,1)S(1)} all-gather(bf16[1,12,16,128]{3,2,1,0:T(8,128)(2,1)S(1)} %bitcast.32), channel_id=1, replica_groups=mesh['z'=16,'x'=4,'y'=8,'core'=2] {'z'}, dimensions={0}, use_global_device_ids=true | all-gather | bytes 835584 | tf_op jit(solution)/shard_map/all_gather | solution.py:184
  77.9 1.0 fusion.2
  78.9 3.1 %collective-permute-start.1 = (bf16[1536,128]{1,0:T(8,128)(2,1)}, bf16[1536,128]{1,0:T(8,128)(2,1)S(1)}, u32[]{:S(2)}, u32[]{:S(2)}) collective-permute-start(bf16[1536,128]{1,0:T(8,128)(2,1)} %bitcast.9), channel_id=1, source_target_pairs={{0,16},{16,0},{32,48},{48,32},{1,17},{17,1},{33,49},{49,33},{2,18}... | collective-permute-start | bytes 1179656 | tf_op jit(solution)/shard_map/ppermute | solution.py:187
  82.0 3.7 %collective-permute-start.4 = (bf16[1536,128]{1,0:T(8,128)(2,1)}, bf16[1536,128]{1,0:T(8,128)(2,1)S(1)}, u32[]{:S(2)}, u32[]{:S(2)}) collective-permute-start(bf16[1536,128]{1,0:T(8,128)(2,1)} %bitcast.10), channel_id=1, source_target_pairs={{0,48},{16,32},{32,16},{48,0},{1,49},{17,33},{33,17},{49,1},{2,50}... | collective-permute-start | bytes 1179656 | tf_op jit(solution)/shard_map/ppermute | solution.py:188
  85.8 2.8 %collective-permute-start.6 = (bf16[1536,128]{1,0:T(8,128)(2,1)}, bf16[1536,128]{1,0:T(8,128)(2,1)}, u32[]{:S(2)}, u32[]{:S(2)}) collective-permute-start(bf16[1536,128]{1,0:T(8,128)(2,1)} %bitcast.9), channel_id=1, source_target_pairs={{0,48},{16,32},{32,16},{48,0},{1,49},{17,33},{33,17},{49,1},{2,50}... | collective-permute-start | bytes 1179656 | tf_op jit(solution)/shard_map/ppermute | solution.py:190
  88.6 1.9 %collective-permute-start.2 = (bf16[1536,128]{1,0:T(8,128)(2,1)}, bf16[1536,128]{1,0:T(8,128)(2,1)}, u32[]{:S(2)}, u32[]{:S(2)}) collective-permute-start(bf16[1536,128]{1,0:T(8,128)(2,1)} %bitcast.10), channel_id=1, source_target_pairs={{0,16},{16,0},{32,48},{48,32},{1,17},{17,1},{33,49},{49,33},{2,18}... | collective-permute-start | bytes 1179656 | tf_op jit(solution)/shard_map/ppermute | solution.py:189
  90.5 0.0 collective-permute-done.1.x1a
  90.5 3.7 %collective-permute-start.3 = (bf16[1536,128]{1,0:T(8,128)(2,1)S(1)}, bf16[1536,128]{1,0:T(8,128)(2,1)}, u32[]{:S(2)}, u32[]{:S(2)}) collective-permute-start(bf16[1536,128]{1,0:T(8,128)(2,1)S(1)} %collective-permute-done.1.x1a), channel_id=1, source_target_pairs={{0,48},{16,32},{32,16},{48,0},{1,49},{17,33},{33,17},{49,1},{2,50}... | collective-permute-start | bytes 1179656 | tf_op jit(solution)/shard_map/ppermute | solution.py:191
  94.2 0.0 collective-permute-done.4.x3b
  94.2 2.8 %collective-permute-start.5 = (bf16[1536,128]{1,0:T(8,128)(2,1)S(1)}, bf16[1536,128]{1,0:T(8,128)(2,1)}, u32[]{:S(2)}, u32[]{:S(2)}) collective-permute-start(bf16[1536,128]{1,0:T(8,128)(2,1)S(1)} %collective-permute-done.4.x3b), channel_id=1, source_target_pairs={{0,16},{16,0},{32,48},{48,32},{1,17},{17,1},{33,49},{49,33},{2,18}... | collective-permute-start | bytes 1179656 | tf_op jit(solution)/shard_map/ppermute | solution.py:192
  97.0 0.0 collective-permute-done.w1
  97.1 0.2 collective-permute-done.6.x3a
  97.2 2.3 %collective-permute-done.2.x1b = bf16[1536,128]{1,0:T(8,128)(2,1)} collective-permute-done((bf16[1536,128]{1,0:T(8,128)(2,1)}, bf16[1536,128]{1,0:T(8,128)(2,1)}, u32[]{:S(2)}, u32[]{:S(2)}) %collective-permute-start.2) | collective-permute-done | bytes 393248 | tf_op jit(solution)/shard_map/ppermute | solution.py:189
  99.5 6.2 %collective-permute-done.3.x2a = bf16[1536,128]{1,0:T(8,128)(2,1)} collective-permute-done((bf16[1536,128]{1,0:T(8,128)(2,1)S(1)}, bf16[1536,128]{1,0:T(8,128)(2,1)}, u32[]{:S(2)}, u32[]{:S(2)}) %collective-permute-start.3) | collective-permute-done | bytes 393248 | tf_op jit(solution)/shard_map/ppermute | solution.py:191
  105.8 0.6 collective-permute-done.5.x2b
  106.4 0.0 copy-done
  106.4 7.3 %main_step.1 = (bf16[128,384]{1,0:T(8,128)(2,1)}, bf16[384,128]{1,0:T(8,128)(2,1)S(1)}, bf16[12288,128]{1,0:T(8,128)(2,1)S(1)}, bf16[8,384,128]{2,1,0:T(8,128)(2,1)S(1)}) custom-call(s32[16,128]{1,0:T(8,128)S(1)} %maximum_convert_fusion.table, s32[1]{0:T(128)} %bitcast.5.here, bf16[3072,128]{1,0:T(8,128)(2,1)S(1)} %bitcast.30, ...), custom_call_target="tpu_custom_call" | custom-call | flops 2000000000 | bytes 8000000 | tf_op jit(solution)/shard_map/main_step/pallas_call | solution.py:127
  113.7 9.8 %collective-permute-start.7 = (bf16[8,384,128]{2,1,0:T(8,128)(2,1)S(1)}, bf16[8,384,128]{2,1,0:T(8,128)(2,1)S(1)}, u32[]{:S(2)}, u32[]{:S(2)}) collective-permute-start(bf16[8,384,128]{2,1,0:T(8,128)(2,1)S(1)} %get-tuple-element.9), channel_id=1, source_target_pairs={{0,1},{1,0},{2,3},{3,2},{4,5},{5,4},{6,7},{7,6},{8,9},{9,8},{10,11... | collective-permute-start | bytes 2359304 | tf_op jit(solution)/shard_map/ppermute | solution.py:200
  123.5 2.2 %rest_step.1 = bf16[8,384,128]{2,1,0:T(8,128)(2,1)S(1)} custom-call(s32[16,128]{1,0:T(8,128)S(1)} %maximum_convert_fusion.table, bf16[12288,128]{1,0:T(8,128)(2,1)S(1)} %get-tuple-element.7.x, bf16[384,128]{1,0:T(8,128)(2,1)S(1)} %get-tuple-element.8.grad_t), custom_call_target="tpu_custom_call" | custom-call | flops 1000000000 | bytes 4000000 | tf_op jit(solution)/shard_map/rest_step/pallas_call | solution.py:150
  125.8 0.0 collective-permute-done.7
  125.8 1.1 add_convert_fusion
  126.9 3.5 %all-to-all-start.1 = ((bf16[8,384,128]{2,1,0:T(8,128)(2,1)}), bf16[8,384,128]{2,1,0:T(8,128)(2,1)S(1)}, u32[]{:S(2)}, u32[]{:S(2)}) async-start(bf16[8,384,128]{2,1,0:T(8,128)(2,1)} %add_convert_fusion), calls=%async_computation.1 | async-start | bytes 1572864 | tf_op jit(solution)/shard_map/all_to_all | solution.py:203
  130.4 23.6 %all-to-all-done.1 = bf16[8,384,128]{2,1,0:T(8,128)(2,1)S(1)} async-done(((bf16[8,384,128]{2,1,0:T(8,128)(2,1)}), bf16[8,384,128]{2,1,0:T(8,128)(2,1)S(1)}, u32[]{:S(2)}, u32[]{:S(2)}) %all-to-all-start.1) | async-done | bytes 786464 | tf_op jit(solution)/shard_map/all_to_all | solution.py:203
  154.0 0.1 convert_reduce_fusion
  154.1 0.1 reshape.231
  154.2 0.2 copy.12
  154.4 0.2 reshape.232
  154.6 0.7 select_convert_fusion
  (6 shorter events, 0.1 us)
Async XLA Ops:
  2.7 36.0 %copy-start.1 = (bf16[128,192]{0,1:T(8,128)(2,1)S(1)}, bf16[128,192]{0,1:T(8,128)(2,1)}, u32[]{:S(2)}) copy-start(bf16[128,192]{0,1:T(8,128)(2,1)} %param.5) | copy-start | bytes 147460
  26.5 79.9 %copy-start = (bf16[128,384]{1,0:T(8,128)(2,1)S(1)}, bf16[128,384]{1,0:T(8,128)(2,1)}, u32[]{:S(2)}) copy-start(bf16[128,384]{1,0:T(8,128)(2,1)} %up.1) | copy-start | bytes 294916
  26.5 70.5 %collective-permute-start = (bf16[8,400,128]{2,1,0:T(8,128)(2,1)S(1)}, bf16[8,400,128]{2,1,0:T(8,128)(2,1)S(1)}, u32[]{:S(2)}, u32[]{:S(2)}) collective-permute-start(bf16[8,400,128]{2,1,0:T(8,128)(2,1)S(1)} %all_to_all.10.w0), channel_id=1, source_target_pairs={{0,1},{1,0},{2,3},{3,2},{4,5},{5,4},{6,7},{7,6},{8,9},{9,8},{10,11... | collective-permute-start | bytes 2457608 | tf_op jit(solution)/shard_map/ppermute | solution.py:193
  78.9 11.6 %collective-permute-start.1 = (bf16[1536,128]{1,0:T(8,128)(2,1)}, bf16[1536,128]{1,0:T(8,128)(2,1)S(1)}, u32[]{:S(2)}, u32[]{:S(2)}) collective-permute-start(bf16[1536,128]{1,0:T(8,128)(2,1)} %bitcast.9), channel_id=1, source_target_pairs={{0,16},{16,0},{32,48},{48,32},{1,17},{17,1},{33,49},{49,33},{2,18}... | collective-permute-start | bytes 1179656 | tf_op jit(solution)/shard_map/ppermute | solution.py:187
  82.0 12.2 %collective-permute-start.4 = (bf16[1536,128]{1,0:T(8,128)(2,1)}, bf16[1536,128]{1,0:T(8,128)(2,1)S(1)}, u32[]{:S(2)}, u32[]{:S(2)}) collective-permute-start(bf16[1536,128]{1,0:T(8,128)(2,1)} %bitcast.10), channel_id=1, source_target_pairs={{0,48},{16,32},{32,16},{48,0},{1,49},{17,33},{33,17},{49,1},{2,50}... | collective-permute-start | bytes 1179656 | tf_op jit(solution)/shard_map/ppermute | solution.py:188
  85.8 11.5 %collective-permute-start.6 = (bf16[1536,128]{1,0:T(8,128)(2,1)}, bf16[1536,128]{1,0:T(8,128)(2,1)}, u32[]{:S(2)}, u32[]{:S(2)}) collective-permute-start(bf16[1536,128]{1,0:T(8,128)(2,1)} %bitcast.9), channel_id=1, source_target_pairs={{0,48},{16,32},{32,16},{48,0},{1,49},{17,33},{33,17},{49,1},{2,50}... | collective-permute-start | bytes 1179656 | tf_op jit(solution)/shard_map/ppermute | solution.py:190
  88.6 11.0 %collective-permute-start.2 = (bf16[1536,128]{1,0:T(8,128)(2,1)}, bf16[1536,128]{1,0:T(8,128)(2,1)}, u32[]{:S(2)}, u32[]{:S(2)}) collective-permute-start(bf16[1536,128]{1,0:T(8,128)(2,1)} %bitcast.10), channel_id=1, source_target_pairs={{0,16},{16,0},{32,48},{48,32},{1,17},{17,1},{33,49},{49,33},{2,18}... | collective-permute-start | bytes 1179656 | tf_op jit(solution)/shard_map/ppermute | solution.py:189
  90.5 15.3 %collective-permute-start.3 = (bf16[1536,128]{1,0:T(8,128)(2,1)S(1)}, bf16[1536,128]{1,0:T(8,128)(2,1)}, u32[]{:S(2)}, u32[]{:S(2)}) collective-permute-start(bf16[1536,128]{1,0:T(8,128)(2,1)S(1)} %collective-permute-done.1.x1a), channel_id=1, source_target_pairs={{0,48},{16,32},{32,16},{48,0},{1,49},{17,33},{33,17},{49,1},{2,50}... | collective-permute-start | bytes 1179656 | tf_op jit(solution)/shard_map/ppermute | solution.py:191
  94.2 12.2 %collective-permute-start.5 = (bf16[1536,128]{1,0:T(8,128)(2,1)S(1)}, bf16[1536,128]{1,0:T(8,128)(2,1)}, u32[]{:S(2)}, u32[]{:S(2)}) collective-permute-start(bf16[1536,128]{1,0:T(8,128)(2,1)S(1)} %collective-permute-done.4.x3b), channel_id=1, source_target_pairs={{0,16},{16,0},{32,48},{48,32},{1,17},{17,1},{33,49},{49,33},{2,18}... | collective-permute-start | bytes 1179656 | tf_op jit(solution)/shard_map/ppermute | solution.py:192
  113.7 12.1 %collective-permute-start.7 = (bf16[8,384,128]{2,1,0:T(8,128)(2,1)S(1)}, bf16[8,384,128]{2,1,0:T(8,128)(2,1)S(1)}, u32[]{:S(2)}, u32[]{:S(2)}) collective-permute-start(bf16[8,384,128]{2,1,0:T(8,128)(2,1)S(1)} %get-tuple-element.9), channel_id=1, source_target_pairs={{0,1},{1,0},{2,3},{3,2},{4,5},{5,4},{6,7},{7,6},{8,9},{9,8},{10,11... | collective-permute-start | bytes 2359304 | tf_op jit(solution)/shard_map/ppermute | solution.py:200
  126.9 27.1 %all-to-all-start.1 = ((bf16[8,384,128]{2,1,0:T(8,128)(2,1)}), bf16[8,384,128]{2,1,0:T(8,128)(2,1)S(1)}, u32[]{:S(2)}, u32[]{:S(2)}) async-start(bf16[8,384,128]{2,1,0:T(8,128)(2,1)} %add_convert_fusion), calls=%async_computation.1 | async-start | bytes 1572864 | tf_op jit(solution)/shard_map/all_to_all | solution.py:203

commit v2 on v1

--- a/solution.py
+++ b/solution.py
@@ -21,6 +21,8 @@
 COL_ROWS = NZ * SHARD
 CUT = COL_ROWS // 2
 X_ROWS = NX * COL_ROWS
+UNITS = COL_ROWS // TILE
+GROUP = 8
 FF_LOC = 384
 TOK = 128
 
@@ -52,53 +54,95 @@
         dw[y, m * TILE : (m + 1) * TILE, :] = jnp.where(low, prod[:TILE], prod[TILE:]).astype(jnp.bfloat16)
 
 
-def main_kernel(
-    table, here, x0, x1a, x1b, x2a, x2b, x3a, x3b, w0, w1, up, out, grad_t, x, dw, acc, tiles0, tiles1, sem
-):
+def lane_masks():
+    low = lanes_below()
+    return jnp.where(low, 1.0, 0.0).astype(jnp.bfloat16), jnp.where(low, 0.0, 1.0).astype(jnp.bfloat16)
+
+
+def early_kernel(table, here, x0, x1a, x1b, x3a, x3b, w0, w1, x, tiles, acc, todo, sem):
+    opposite = here[0] ^ 2
+    x[pl.ds(pl.multiple_of(opposite * COL_ROWS, COL_ROWS), COL_ROWS), :] = jnp.zeros((COL_ROWS, TOK), jnp.bfloat16)
+
     def part(distance, start, size):
         column = here[0] ^ distance
         return x.at[pl.ds(pl.multiple_of(column * COL_ROWS + start, CUT), size), :]
 
     moves = [
-        (w0, tiles0),
-        (w1, tiles1),
         (x0, part(0, 0, COL_ROWS)),
         (x1a, part(1, 0, CUT)),
         (x1b, part(1, CUT, CUT)),
-        (x2a, part(2, 0, CUT)),
-        (x2b, part(2, CUT, CUT)),
         (x3a, part(3, 0, CUT)),
         (x3b, part(3, CUT, CUT)),
+        (w0, tiles.at[0:NY]),
+        (w1, tiles.at[NY : 2 * NY]),
     ]
     copies = [pltpu.make_async_copy(a, b, sem.at[i]) for i, (a, b) in enumerate(moves)]
     for c in copies:
         c.start()
     acc[...] = jnp.zeros_like(acc)
-    for c in copies[2:]:
+
+    def sort_out(b, n):
+        for s in range(CAP):
+            todo[0, n] = b * 16 + s
+            todo[1, n] = table[b, F_LANE + s]
+            ahead = table[b, s] - opposite * UNITS
+            n = n + jnp.where((ahead >= 0) & (ahead < UNITS), 1, 0)
+        return n
+
+    count = lax.fori_loop(0, 2 * NY, sort_out, 0)
+    for i in range(GROUP):
+        todo[0, count + i] = 0
+        todo[1, count + i] = PER_COL
+    todo[2, 0] = count
+    first, second = lane_masks()
+    for c in copies:
         c.wait()
-    low = lanes_below()
-    first = jnp.where(low, 1.0, 0.0).astype(jnp.bfloat16)
-    second = jnp.where(low, 0.0, 1.0).astype(jnp.bfloat16)
-    for rc, tiles in enumerate((tiles0, tiles1)):
-        copies[rc].wait()
-
-        def forward(y, carry, rc=rc, tiles=tiles):
-            b = rc * NY + y
-            for m in range(PAIRS):
-                s = 2 * m
-                tile = tiles[y, m * TILE : (m + 1) * TILE, :]
-                prod = jnp.dot(
-                    jnp.concatenate([tile * first, tile * second], axis=0),
-                    two(x, table[b, s], table[b, s + 1]),
-                    preferred_element_type=jnp.float32,
-                )
-                for p in range(2):
-                    acc[aligned(table[b, F_LANE + s + p] * TILE, TILE), :] += prod[p * TILE : (p + 1) * TILE]
-            return carry
-
-        lax.fori_loop(0, NY, forward, 0, unroll=2)
-
-    pre = acc[...].T
+
+    def forward(b, carry):
+        for m in range(PAIRS):
+            s = 2 * m
+            tile = tiles[b, m * TILE : (m + 1) * TILE, :]
+            prod = jnp.dot(
+                jnp.concatenate([tile * first, tile * second], axis=0),
+                two(x, table[b, s], table[b, s + 1]),
+                preferred_element_type=jnp.float32,
+            )
+            for p in range(2):
+                acc[aligned(table[b, F_LANE + s + p] * TILE, TILE), :] += prod[p * TILE : (p + 1) * TILE]
+        return carry
+
+    lax.fori_loop(0, 2 * NY, forward, 0, unroll=2)
+
+
+def main_kernel(table, here, todo, x_in, tiles, acc_in, x2a, x2b, up, out, grad_t, x, dw, acc, sem):
+    base = (here[0] ^ 2) * COL_ROWS
+    copies = [
+        pltpu.make_async_copy(x2a, x.at[pl.ds(pl.multiple_of(base, CUT), CUT), :], sem.at[0]),
+        pltpu.make_async_copy(x2b, x.at[pl.ds(pl.multiple_of(base + CUT, CUT), CUT), :], sem.at[1]),
+    ]
+    for c in copies:
+        c.start()
+    acc[...] = acc_in[...]
+    first, second = lane_masks()
+    for c in copies:
+        c.wait()
+
+    def forward(g, carry):
+        for i in range(GROUP):
+            j = todo[0, g * GROUP + i]
+            b, s = j >> 4, j & 15
+            m = s >> 1
+            tile = tiles[b, aligned(m * TILE, TILE), :]
+            prod = jnp.dot(
+                tile * jnp.where((s & 1) == 0, first, second),
+                two(x, table[b, 2 * m], table[b, 2 * m + 1]),
+                preferred_element_type=jnp.float32,
+            )
+            acc[aligned(todo[1, g * GROUP + i] * TILE, TILE), :] += prod
+        return carry
+
+    lax.fori_loop(0, (todo[2, 0] + GROUP - 1) // GROUP, forward, 0)
+    pre = acc[:FF_LOC].T
     cumul = 0.5 * (1.0 + lax.erf(pre * 0.7071067811865476))
     density = jnp.exp(-0.5 * pre * pre) * 0.3989422804014327
     out[...] = (pre * cumul).astype(jnp.bfloat16)
@@ -123,7 +167,25 @@
     return pltpu.CompilerParams(vmem_limit_bytes=mib << 20)
 
 
-def main_step(table, here, x0, x1a, x1b, x2a, x2b, x3a, x3b, w0, w1, up):
+def early_step(table, here, *parts):
+    return pl.pallas_call(
+        early_kernel,
+        out_shape=(
+            jax.ShapeDtypeStruct((X_ROWS, TOK), jnp.bfloat16),
+            jax.ShapeDtypeStruct((2 * NY, ROWS, PAIR), jnp.bfloat16),
+            jax.ShapeDtypeStruct((FF_LOC + TILE, TOK), jnp.float32),
+            jax.ShapeDtypeStruct((3, 256), jnp.int32),
+        ),
+        in_specs=[SMEM, SMEM] + [ANY] * 7,
+        out_specs=(VMEM, VMEM, VMEM, SMEM),
+        scratch_shapes=[pltpu.SemaphoreType.DMA((7,))],
+        compiler_params=params(12),
+        cost_estimate=pl.CostEstimate(flops=10**9, bytes_accessed=8 * 10**6, transcendentals=0),
+        name="early_step",
+    )(table, here, *parts)
+
+
+def main_step(table, here, todo, x, tiles, acc, x2a, x2b, up):
     return pl.pallas_call(
         main_kernel,
         out_shape=(
@@ -132,18 +194,14 @@
             jax.ShapeDtypeStruct((X_ROWS, TOK), jnp.bfloat16),
             jax.ShapeDtypeStruct((NY, PACK, PAIR), jnp.bfloat16),
         ),
-        in_specs=[SMEM, SMEM] + [ANY] * 9 + [VMEM],
+        in_specs=[SMEM, SMEM, SMEM, VMEM, VMEM, VMEM, ANY, ANY, VMEM],
         out_specs=(VMEM, VMEM, VMEM, VMEM),
-        scratch_shapes=[
-            pltpu.VMEM((FF_LOC, TOK), jnp.float32),
-            pltpu.VMEM((NY, ROWS, PAIR), jnp.bfloat16),
-            pltpu.VMEM((NY, ROWS, PAIR), jnp.bfloat16),
-            pltpu.SemaphoreType.DMA((9,)),
-        ],
-        compiler_params=params(16),
-        cost_estimate=pl.CostEstimate(flops=2 * 10**9, bytes_accessed=8 * 10**6, transcendentals=10**5),
+        scratch_shapes=[pltpu.VMEM((FF_LOC + TILE, TOK), jnp.float32), pltpu.SemaphoreType.DMA((2,))],
+        input_output_aliases={3: 2},
+        compiler_params=params(14),
+        cost_estimate=pl.CostEstimate(flops=10**9, bytes_accessed=8 * 10**6, transcendentals=10**5),
         name="main_step",
-    )(table, here, x0, x1a, x1b, x2a, x2b, x3a, x3b, w0, w1, up)
+    )(table, here, todo, x, tiles, acc, x2a, x2b, up)
 
 
 def rest_step(table, x, grad_t):
@@ -196,7 +254,8 @@
         [jnp.sum(w[:, PACK:, :].astype(jnp.float32), axis=1) for w in (w_own, w_other)], axis=0
     ).astype(jnp.int32)
     here = lax.axis_index("x").astype(jnp.int32).reshape(1)
-    output, grad, x, theirs = main_step(table, here, x0, x1a, x1b, x2a, x2b, x3a, x3b, w_own, w_other, upstream)
+    x, tiles, acc, todo = early_step(table, here, x0, x1a, x1b, x3a, x3b, w_own, w_other)
+    output, grad, x, theirs = main_step(table, here, todo, x, tiles, acc, x2a, x2b, upstream)
     arrived = lax.ppermute(theirs, "core", SWAP)
     mine = rest_step(table, x, grad)
     both = (mine.astype(jnp.float32) + arrived.astype(jnp.float32)).astype(jnp.bfloat16)

time: 156 us -> 155 us (level)
  waiting for transfers between devices: 32.9 us -> 27.2 us
  Pallas kernels: 9.52 us -> 13 us
    ppermute x1, waiting for transfers between devices: 6.24 us -> 0.53 us  [body(): x2a = lax.ppermute(x1a, 'x', far)]
    pallas_call x0 -> x1, Pallas kernels: none -> 5.7 us  [early_step(): pl.pallas_call(early_kernel, out_shape=(jax.ShapeDtypeStruct((X_ROWS, TOK...]
    pallas_call x1, Pallas kernels: 7.28 us -> 5.09 us  [main_step(): pl.pallas_call(main_kernel, out_shape=(jax.ShapeDtypeStruct((TOK, FF_LOC)...]
  transfers between devices with their start and end apart: 9 -> 9, of which waited for: 5 -> 5; matrix products, arithmetic and copies ran while one was open for 1% -> 1% of each run, Pallas kernels for 1% -> 5%
where the time goes in v2:
time: 155 us; the launch traced here: 154 us
  blocking collectives  62 us (40%)
  starting transfers between devices  44.5 us (29%)
  waiting for transfers between devices  27.2 us (18%)
  Pallas kernels  13 us (8%)
  local copies, waits for them, and re-layouts  3.01 us (2%)
  other arithmetic  2.84 us (2%)
    all_gather x1, blocking collectives, body(): x0 = lax.all_gather(x_mine, 'z', axis=0, tiled=True).reshape(COL_ROWS, TOK)  39.2 us
    all_to_all x1, waiting for transfers between devices, body(): parts = lax.all_to_all(both, 'y', split_axis=0, concat_axis=0, tiled=True)  23.6 us
    all_to_all x1, blocking collectives, body(): w_own = lax.all_to_all(wide, 'y', split_axis=0, concat_axis=0, tiled=True)  22.8 us
    ppermute x1, starting transfers between devices, body(): w_other = lax.ppermute(w_own, 'core', SWAP)  12 us
    ppermute x1, starting transfers between devices, body(): arrived = lax.ppermute(theirs, 'core', SWAP)  10.9 us
    pallas_call x1, Pallas kernels, early_step(): pl.pallas_call(early_kernel, out_shape=(jax.ShapeDtypeStruct((X_ROWS, TOK...  5.7 us
    pallas_call x1, Pallas kernels, main_step(): pl.pallas_call(main_kernel, out_shape=(jax.ShapeDtypeStruct((TOK, FF_LOC)...  5.09 us
    ppermute x1, starting transfers between devices, body(): x2a = lax.ppermute(x1a, 'x', far)  3.72 us
  transfers between devices with their start and end apart: 9, of which 5 were waited for; matrix products, arithmetic and copies ran while one was open for 1% of the time, Pallas kernels for 5%

profile of v2, /device:TPU:1, one launch (start us, length us, event | category | flops | bytes accessed | tf_op | source)
XLA Modules:
  0.0 154.1 jit_solution(15742833709564034811)
XLA Ops:
  1.3 1.1 reshape.226
  2.4 0.1 select_bitcast_fusion
  2.5 0.1 copy.12
  2.7 0.0 copy-start.1
  2.7 0.1 reshape.227
  2.8 0.7 fusion.1
  3.5 0.1 add_convert_fusion.1
  3.6 0.1 broadcast_in_dim.34
  3.7 22.8 %all_to_all.10.w0 = bf16[8,400,128]{2,1,0:T(8,128)(2,1)S(1)} all-to-all(bf16[8,400,128]{2,1,0:T(8,128)(2,1)S(1)} %broadcast_in_dim.34), channel_id=1, replica_groups=mesh['z'=16,'x'=4,'y'=8,'core'=2] {'y'}, dimensions={0} | all-to-all | bytes 1638400 | tf_op jit(solution)/shard_map/all_to_all | solution.py:239
  26.5 12.0 %collective-permute-start = (bf16[8,400,128]{2,1,0:T(8,128)(2,1)S(1)}, bf16[8,400,128]{2,1,0:T(8,128)(2,1)S(1)}, u32[]{:S(2)}, u32[]{:S(2)}) collective-permute-start(bf16[8,400,128]{2,1,0:T(8,128)(2,1)S(1)} %all_to_all.10.w0), channel_id=1, source_target_pairs={{0,1},{1,0},{2,3},{3,2},{4,5},{5,4},{6,7},{7,6},{8,9},{9,8},{10,11... | collective-permute-start | bytes 2457608 | tf_op jit(solution)/shard_map/ppermute | solution.py:251
  38.6 0.0 copy-done.1
  38.6 39.2 %all_gather.3 = bf16[16,12,16,128]{3,2,1,0:T(8,128)(2,1)S(1)} all-gather(bf16[1,12,16,128]{3,2,1,0:T(8,128)(2,1)S(1)} %bitcast.32), channel_id=1, replica_groups=mesh['z'=16,'x'=4,'y'=8,'core'=2] {'z'}, dimensions={0}, use_global_device_ids=true | all-gather | bytes 835584 | tf_op jit(solution)/shard_map/all_gather | solution.py:242
  77.8 1.0 fusion.2
  78.8 3.1 %collective-permute-start.1 = (bf16[1536,128]{1,0:T(8,128)(2,1)}, bf16[1536,128]{1,0:T(8,128)(2,1)S(1)}, u32[]{:S(2)}, u32[]{:S(2)}) collective-permute-start(bf16[1536,128]{1,0:T(8,128)(2,1)} %bitcast.9), channel_id=1, source_target_pairs={{0,16},{16,0},{32,48},{48,32},{1,17},{17,1},{33,49},{49,33},{2,18}... | collective-permute-start | bytes 1179656 | tf_op jit(solution)/shard_map/ppermute | solution.py:245
  81.9 3.7 %collective-permute-start.4 = (bf16[1536,128]{1,0:T(8,128)(2,1)}, bf16[1536,128]{1,0:T(8,128)(2,1)S(1)}, u32[]{:S(2)}, u32[]{:S(2)}) collective-permute-start(bf16[1536,128]{1,0:T(8,128)(2,1)} %bitcast.10), channel_id=1, source_target_pairs={{0,48},{16,32},{32,16},{48,0},{1,49},{17,33},{33,17},{49,1},{2,50}... | collective-permute-start | bytes 1179656 | tf_op jit(solution)/shard_map/ppermute | solution.py:246
  85.6 2.8 %collective-permute-start.3 = (bf16[1536,128]{1,0:T(8,128)(2,1)}, bf16[1536,128]{1,0:T(8,128)(2,1)}, u32[]{:S(2)}, u32[]{:S(2)}) collective-permute-start(bf16[1536,128]{1,0:T(8,128)(2,1)} %bitcast.9), channel_id=1, source_target_pairs={{0,48},{16,32},{32,16},{48,0},{1,49},{17,33},{33,17},{49,1},{2,50}... | collective-permute-start | bytes 1179656 | tf_op jit(solution)/shard_map/ppermute | solution.py:248
  88.4 1.9 %collective-permute-start.2 = (bf16[1536,128]{1,0:T(8,128)(2,1)}, bf16[1536,128]{1,0:T(8,128)(2,1)}, u32[]{:S(2)}, u32[]{:S(2)}) collective-permute-start(bf16[1536,128]{1,0:T(8,128)(2,1)} %bitcast.10), channel_id=1, source_target_pairs={{0,16},{16,0},{32,48},{48,32},{1,17},{17,1},{33,49},{49,33},{2,18}... | collective-permute-start | bytes 1179656 | tf_op jit(solution)/shard_map/ppermute | solution.py:247
  90.3 0.0 collective-permute-done.1.x1a
  90.3 3.7 %collective-permute-start.5 = (bf16[1536,128]{1,0:T(8,128)(2,1)S(1)}, bf16[1536,128]{1,0:T(8,128)(2,1)S(1)}, u32[]{:S(2)}, u32[]{:S(2)}) collective-permute-start(bf16[1536,128]{1,0:T(8,128)(2,1)S(1)} %collective-permute-done.1.x1a), channel_id=1, source_target_pairs={{0,48},{16,32},{32,16},{48,0},{1,49},{17,33},{33,17},{49,1},{2,50}... | collective-permute-start | bytes 1179656 | tf_op jit(solution)/shard_map/ppermute | solution.py:249
  94.1 0.0 collective-permute-done.4.x3b
  94.1 2.8 %collective-permute-start.6 = (bf16[1536,128]{1,0:T(8,128)(2,1)S(1)}, bf16[1536,128]{1,0:T(8,128)(2,1)S(1)}, u32[]{:S(2)}, u32[]{:S(2)}) collective-permute-start(bf16[1536,128]{1,0:T(8,128)(2,1)S(1)} %collective-permute-done.4.x3b), channel_id=1, source_target_pairs={{0,16},{16,0},{32,48},{48,32},{1,17},{17,1},{33,49},{49,33},{2,18}... | collective-permute-start | bytes 1179656 | tf_op jit(solution)/shard_map/ppermute | solution.py:250
  96.9 0.0 collective-permute-done.w1
  96.9 0.2 collective-permute-done.3.x3a
  97.1 2.3 %collective-permute-done.2.x1b = bf16[1536,128]{1,0:T(8,128)(2,1)} collective-permute-done((bf16[1536,128]{1,0:T(8,128)(2,1)}, bf16[1536,128]{1,0:T(8,128)(2,1)}, u32[]{:S(2)}, u32[]{:S(2)}) %collective-permute-start.2) | collective-permute-done | bytes 393248 | tf_op jit(solution)/shard_map/ppermute | solution.py:247
  99.4 0.0 copy-start
  99.4 5.7 %early_step.1 = (bf16[12288,128]{1,0:T(8,128)(2,1)S(1)}, bf16[16,400,128]{2,1,0:T(8,128)(2,1)S(1)}, f32[448,128]{1,0:T(8,128)S(1)}, s32[3,256]{1,0:T(4,128)S(1)}) custom-call(s32[16,128]{1,0:T(8,128)S(1)} %maximum_convert_fusion.table, s32[1]{0:T(128)} %bitcast.5.here, bf16[3072,128]{1,0:T(8,128)(2,1)S(1)} %bitcast.30, ...), custom_call_target="tpu_custom_call" | custom-call | flops 1000000000 | bytes 8000000 | tf_op jit(solution)/shard_map/early_step/pallas_call | solution.py:171
  105.1 0.5 collective-permute-done.5.x2a
  105.6 0.6 collective-permute-done.6.x2b
  106.3 0.0 copy-done
  106.3 5.1 %main_step.1 = (bf16[128,384]{1,0:T(8,128)(2,1)}, bf16[384,128]{1,0:T(8,128)(2,1)S(1)}, bf16[12288,128]{1,0:T(8,128)(2,1)S(1)}, bf16[8,384,128]{2,1,0:T(8,128)(2,1)S(1)}) custom-call(s32[16,128]{1,0:T(8,128)S(1)} %maximum_convert_fusion.table, s32[1]{0:T(128)} %bitcast.5.here, s32[3,256]{1,0:T(4,128)S(1)} %get-tuple-element.10.todo, ...), custom_call_target="tpu_custom_call", output_to_operand_aliasing={{2}: (3, {})} | custom-call | flops 1000000000 | bytes 8000000 | tf_op jit(solution)/shard_map/main_step/pallas_call | solution.py:189
  111.4 10.9 %collective-permute-start.7 = (bf16[8,384,128]{2,1,0:T(8,128)(2,1)S(1)}, bf16[8,384,128]{2,1,0:T(8,128)(2,1)S(1)}, u32[]{:S(2)}, u32[]{:S(2)}) collective-permute-start(bf16[8,384,128]{2,1,0:T(8,128)(2,1)S(1)} %get-tuple-element.17), channel_id=1, source_target_pairs={{0,1},{1,0},{2,3},{3,2},{4,5},{5,4},{6,7},{7,6},{8,9},{9,8},{10,11... | collective-permute-start | bytes 2359304 | tf_op jit(solution)/shard_map/ppermute | solution.py:259
  122.3 2.2 %rest_step.1 = bf16[8,384,128]{2,1,0:T(8,128)(2,1)S(1)} custom-call(s32[16,128]{1,0:T(8,128)S(1)} %maximum_convert_fusion.table, bf16[12288,128]{1,0:T(8,128)(2,1)S(1)} %get-tuple-element.15.x, bf16[384,128]{1,0:T(8,128)(2,1)S(1)} %get-tuple-element.16.grad_t), custom_call_target="tpu_custom_call" | custom-call | flops 1000000000 | bytes 4000000 | tf_op jit(solution)/shard_map/rest_step/pallas_call | solution.py:208
  124.5 0.0 collective-permute-done.7
  124.5 1.1 add_convert_fusion
  125.6 3.5 %all-to-all-start.1 = ((bf16[8,384,128]{2,1,0:T(8,128)(2,1)}), bf16[8,384,128]{2,1,0:T(8,128)(2,1)S(1)}, u32[]{:S(2)}, u32[]{:S(2)}) async-start(bf16[8,384,128]{2,1,0:T(8,128)(2,1)} %add_convert_fusion), calls=%async_computation.1 | async-start | bytes 1572864 | tf_op jit(solution)/shard_map/all_to_all | solution.py:262
  129.2 23.6 %all-to-all-done.1 = bf16[8,384,128]{2,1,0:T(8,128)(2,1)S(1)} async-done(((bf16[8,384,128]{2,1,0:T(8,128)(2,1)}), bf16[8,384,128]{2,1,0:T(8,128)(2,1)S(1)}, u32[]{:S(2)}, u32[]{:S(2)}) %all-to-all-start.1) | async-done | bytes 786464 | tf_op jit(solution)/shard_map/all_to_all | solution.py:262
  152.8 0.1 convert_reduce_fusion
  152.9 0.1 reshape.231
  153.0 0.2 copy.13
  153.1 0.2 reshape.232
  153.3 0.7 select_convert_fusion
  (6 shorter events, 0.1 us)
Async XLA Ops:
  2.7 35.9 %copy-start.1 = (bf16[128,192]{0,1:T(8,128)(2,1)S(1)}, bf16[128,192]{0,1:T(8,128)(2,1)}, u32[]{:S(2)}) copy-start(bf16[128,192]{0,1:T(8,128)(2,1)} %param.5) | copy-start | bytes 147460
  26.5 70.3 %collective-permute-start = (bf16[8,400,128]{2,1,0:T(8,128)(2,1)S(1)}, bf16[8,400,128]{2,1,0:T(8,128)(2,1)S(1)}, u32[]{:S(2)}, u32[]{:S(2)}) collective-permute-start(bf16[8,400,128]{2,1,0:T(8,128)(2,1)S(1)} %all_to_all.10.w0), channel_id=1, source_target_pairs={{0,1},{1,0},{2,3},{3,2},{4,5},{5,4},{6,7},{7,6},{8,9},{9,8},{10,11... | collective-permute-start | bytes 2457608 | tf_op jit(solution)/shard_map/ppermute | solution.py:251
  78.8 11.6 %collective-permute-start.1 = (bf16[1536,128]{1,0:T(8,128)(2,1)}, bf16[1536,128]{1,0:T(8,128)(2,1)S(1)}, u32[]{:S(2)}, u32[]{:S(2)}) collective-permute-start(bf16[1536,128]{1,0:T(8,128)(2,1)} %bitcast.9), channel_id=1, source_target_pairs={{0,16},{16,0},{32,48},{48,32},{1,17},{17,1},{33,49},{49,33},{2,18}... | collective-permute-start | bytes 1179656 | tf_op jit(solution)/shard_map/ppermute | solution.py:245
  81.9 12.2 %collective-permute-start.4 = (bf16[1536,128]{1,0:T(8,128)(2,1)}, bf16[1536,128]{1,0:T(8,128)(2,1)S(1)}, u32[]{:S(2)}, u32[]{:S(2)}) collective-permute-start(bf16[1536,128]{1,0:T(8,128)(2,1)} %bitcast.10), channel_id=1, source_target_pairs={{0,48},{16,32},{32,16},{48,0},{1,49},{17,33},{33,17},{49,1},{2,50}... | collective-permute-start | bytes 1179656 | tf_op jit(solution)/shard_map/ppermute | solution.py:246
  85.6 11.5 %collective-permute-start.3 = (bf16[1536,128]{1,0:T(8,128)(2,1)}, bf16[1536,128]{1,0:T(8,128)(2,1)}, u32[]{:S(2)}, u32[]{:S(2)}) collective-permute-start(bf16[1536,128]{1,0:T(8,128)(2,1)} %bitcast.9), channel_id=1, source_target_pairs={{0,48},{16,32},{32,16},{48,0},{1,49},{17,33},{33,17},{49,1},{2,50}... | collective-permute-start | bytes 1179656 | tf_op jit(solution)/shard_map/ppermute | solution.py:248
  88.4 11.0 %collective-permute-start.2 = (bf16[1536,128]{1,0:T(8,128)(2,1)}, bf16[1536,128]{1,0:T(8,128)(2,1)}, u32[]{:S(2)}, u32[]{:S(2)}) collective-permute-start(bf16[1536,128]{1,0:T(8,128)(2,1)} %bitcast.10), channel_id=1, source_target_pairs={{0,16},{16,0},{32,48},{48,32},{1,17},{17,1},{33,49},{49,33},{2,18}... | collective-permute-start | bytes 1179656 | tf_op jit(solution)/shard_map/ppermute | solution.py:247
  90.3 15.3 %collective-permute-start.5 = (bf16[1536,128]{1,0:T(8,128)(2,1)S(1)}, bf16[1536,128]{1,0:T(8,128)(2,1)S(1)}, u32[]{:S(2)}, u32[]{:S(2)}) collective-permute-start(bf16[1536,128]{1,0:T(8,128)(2,1)S(1)} %collective-permute-done.1.x1a), channel_id=1, source_target_pairs={{0,48},{16,32},{32,16},{48,0},{1,49},{17,33},{33,17},{49,1},{2,50}... | collective-permute-start | bytes 1179656 | tf_op jit(solution)/shard_map/ppermute | solution.py:249
  94.1 12.2 %collective-permute-start.6 = (bf16[1536,128]{1,0:T(8,128)(2,1)S(1)}, bf16[1536,128]{1,0:T(8,128)(2,1)S(1)}, u32[]{:S(2)}, u32[]{:S(2)}) collective-permute-start(bf16[1536,128]{1,0:T(8,128)(2,1)S(1)} %collective-permute-done.4.x3b), channel_id=1, source_target_pairs={{0,16},{16,0},{32,48},{48,32},{1,17},{17,1},{33,49},{49,33},{2,18}... | collective-permute-start | bytes 1179656 | tf_op jit(solution)/shard_map/ppermute | solution.py:250
  99.4 6.9 %copy-start = (bf16[128,384]{1,0:T(8,128)(2,1)S(1)}, bf16[128,384]{1,0:T(8,128)(2,1)}, u32[]{:S(2)}) copy-start(bf16[128,384]{1,0:T(8,128)(2,1)} %up.1) | copy-start | bytes 294916
  111.4 13.2 %collective-permute-start.7 = (bf16[8,384,128]{2,1,0:T(8,128)(2,1)S(1)}, bf16[8,384,128]{2,1,0:T(8,128)(2,1)S(1)}, u32[]{:S(2)}, u32[]{:S(2)}) collective-permute-start(bf16[8,384,128]{2,1,0:T(8,128)(2,1)S(1)} %get-tuple-element.17), channel_id=1, source_target_pairs={{0,1},{1,0},{2,3},{3,2},{4,5},{5,4},{6,7},{7,6},{8,9},{9,8},{10,11... | collective-permute-start | bytes 2359304 | tf_op jit(solution)/shard_map/ppermute | solution.py:259
  125.6 27.1 %all-to-all-start.1 = ((bf16[8,384,128]{2,1,0:T(8,128)(2,1)}), bf16[8,384,128]{2,1,0:T(8,128)(2,1)S(1)}, u32[]{:S(2)}, u32[]{:S(2)}) async-start(bf16[8,384,128]{2,1,0:T(8,128)(2,1)} %add_convert_fusion), calls=%async_computation.1 | async-start | bytes 1572864 | tf_op jit(solution)/shard_map/all_to_all | solution.py:262

commit v3 on v2

--- a/solution.py
+++ b/solution.py
@@ -59,6 +59,29 @@
     return jnp.where(low, 1.0, 0.0).astype(jnp.bfloat16), jnp.where(low, 0.0, 1.0).astype(jnp.bfloat16)
 
 
+def pack_kernel(ids, count, tiles, wide, sent, sem):
+    for m in range(PAIRS):
+        halves = [
+            jnp.where(2 * m + p < count[0, 0], tiles[2 * m + p].astype(jnp.float32).T, 0.0) for p in range(2)
+        ]
+        sent[m * TILE : (m + 1) * TILE, :] = jnp.concatenate(halves, axis=1).astype(jnp.bfloat16)
+    block = 2 * lax.axis_index("y") + lax.axis_index("core")
+    row = lax.broadcasted_iota(jnp.int32, (META, PAIR), 0)
+    lane = lax.broadcasted_iota(jnp.int32, (META, PAIR), 1)
+    meta = jnp.zeros((META, PAIR), jnp.int32)
+    for s in range(CAP):
+        d = (ids[0, s] * 43) >> 8
+        column = (d * 86) >> 8
+        meta = jnp.where(lane == s, column * UNITS + block * SUB + d - column * SUB, meta)
+        meta = jnp.where(lane == F_LANE + s, ids[0, s] - d * PER_COL, meta)
+    sent[PACK:, :] = jnp.where(row == 0, meta, 0).astype(jnp.float32).astype(jnp.bfloat16)
+    copies = [pltpu.make_async_copy(sent, wide.at[y], sem.at[y]) for y in range(NY)]
+    for c in copies:
+        c.start()
+    for c in copies:
+        c.wait()
+
+
 def early_kernel(table, here, x0, x1a, x1b, x3a, x3b, w0, w1, x, tiles, acc, todo, sem):
     opposite = here[0] ^ 2
     x[pl.ds(pl.multiple_of(opposite * COL_ROWS, COL_ROWS), COL_ROWS), :] = jnp.zeros((COL_ROWS, TOK), jnp.bfloat16)
@@ -111,7 +134,7 @@
                 acc[aligned(table[b, F_LANE + s + p] * TILE, TILE), :] += prod[p * TILE : (p + 1) * TILE]
         return carry
 
-    lax.fori_loop(0, 2 * NY, forward, 0, unroll=2)
+    lax.fori_loop(0, 2 * NY, forward, 0, unroll=4)
 
 
 def main_kernel(table, here, todo, x_in, tiles, acc_in, x2a, x2b, up, out, grad_t, x, dw, acc, sem):
@@ -152,7 +175,7 @@
         slot_grads(table, NY + y, x, grad_t, dw, y)
         return carry
 
-    lax.fori_loop(0, NY, backward, 0, unroll=2)
+    lax.fori_loop(0, NY, backward, 0, unroll=4)
 
 
 def rest_kernel(table, x, grad_t, dw):
@@ -160,11 +183,24 @@
         slot_grads(table, y, x, grad_t, dw, y)
         return carry
 
-    lax.fori_loop(0, NY, backward, 0, unroll=2)
+    lax.fori_loop(0, NY, backward, 0, unroll=4)
 
 
 def params(mib):
     return pltpu.CompilerParams(vmem_limit_bytes=mib << 20)
+
+
+def pack_step(ids, count, tiles):
+    return pl.pallas_call(
+        pack_kernel,
+        out_shape=jax.ShapeDtypeStruct((NY, ROWS, PAIR), jnp.bfloat16),
+        in_specs=[SMEM, SMEM, VMEM],
+        out_specs=ANY,
+        scratch_shapes=[pltpu.VMEM((ROWS, PAIR), jnp.bfloat16), pltpu.SemaphoreType.DMA((NY,))],
+        compiler_params=params(4),
+        cost_estimate=pl.CostEstimate(flops=10**5, bytes_accessed=10**6, transcendentals=0),
+        name="pack_step",
+    )(ids, count, tiles)
 
 
 def early_step(table, here, *parts):
@@ -225,17 +261,7 @@
 
 def body(activations, weight_tiles, tile_ids, tile_counts, upstream):
     live = jnp.arange(CAP, dtype=jnp.int32) < tile_counts.reshape(())
-    tiles = jnp.where(live[:, None, None], weight_tiles.reshape(CAP, TILE, TILE), 0)
-    packed = tiles.reshape(PAIRS, 2, TILE, TILE).transpose(0, 3, 1, 2).reshape(PACK, PAIR)
-    ids = tile_ids.reshape(1, CAP)
-    block = 2 * lax.axis_index("y") + lax.axis_index("core")
-    d = ids // PER_COL
-    unit = d // SUB * (NZ * SUB) + block * SUB + d % SUB
-    meta = jnp.pad(unit, ((0, META - 1), (0, PAIR - CAP))) + jnp.pad(
-        ids % PER_COL, ((0, META - 1), (F_LANE, PAIR - F_LANE - CAP))
-    )
-    sent = jnp.concatenate([packed, meta.astype(jnp.bfloat16)], axis=0)
-    wide = jnp.broadcast_to(sent[None], (NY, ROWS, PAIR))
+    wide = pack_step(tile_ids.reshape(1, CAP), tile_counts, weight_tiles.reshape(CAP, TILE, TILE))
     w_own = lax.all_to_all(wide, "y", split_axis=0, concat_axis=0, tiled=True)
 
     x_mine = activations.T.reshape(1, SHARD // 16, 16, TOK)

time: 155 us -> 155 us (level)
    pallas_call x0 -> x1, Pallas kernels: none -> 1.91 us  [pack_step(): pl.pallas_call(pack_kernel, out_shape=jax.ShapeDtypeStruct((NY, ROWS, PAI...]
where the time goes in v3:
time: 155 us; the launch traced here: 154 us
  blocking collectives  62 us (40%)
  starting transfers between devices  43.9 us (28%)
  waiting for transfers between devices  27.8 us (18%)
  Pallas kernels  13.8 us (9%)
  local copies, waits for them, and re-layouts  3.27 us (2%)
  other arithmetic  1.98 us (1%)
    all_gather x1, blocking collectives, body(): x0 = lax.all_gather(x_mine, 'z', axis=0, tiled=True).reshape(COL_ROWS, TOK)  39.2 us
    all_to_all x1, waiting for transfers between devices, body(): parts = lax.all_to_all(both, 'y', split_axis=0, concat_axis=0, tiled=True)  23.5 us
    all_to_all x1, blocking collectives, body(): w_own = lax.all_to_all(wide, 'y', split_axis=0, concat_axis=0, tiled=True)  22.8 us
    ppermute x1, starting transfers between devices, body(): w_other = lax.ppermute(w_own, 'core', SWAP)  12 us
    ppermute x1, starting transfers between devices, body(): arrived = lax.ppermute(theirs, 'core', SWAP)  10.3 us
    pallas_call x1, Pallas kernels, early_step(): pl.pallas_call(early_kernel, out_shape=(jax.ShapeDtypeStruct((X_ROWS, TOK...  5.11 us
    pallas_call x1, Pallas kernels, main_step(): pl.pallas_call(main_kernel, out_shape=(jax.ShapeDtypeStruct((TOK, FF_LOC)...  4.81 us
    ppermute x1, starting transfers between devices, body(): x2a = lax.ppermute(x1a, 'x', far)  3.72 us
  transfers between devices with their start and end apart: 9, of which 5 were waited for; matrix products, arithmetic and copies ran while one was open for 1% of the time, Pallas kernels for 5%

profile of v3, /device:TPU:1, one launch (start us, length us, event | category | flops | bytes accessed | tf_op | source)
XLA Modules:
  0.0 154.2 jit_solution(1018763044624475192)
XLA Ops:
  0.6 0.0 copy-start.2
  1.3 1.1 reshape.68.tiles
  2.4 0.0 copy-start.1
  2.4 0.6 copy-done.1
  3.1 1.9 %pack_step.1 = bf16[8,400,128]{2,1,0:T(8,128)(2,1)S(1)} custom-call(s32[1,12]{1,0:T(1,128)S(1)} %bitcast.14, s32[1,1]{1,0:T(1,128)} %copy.11.count, bf16[12,64,64]{2,1,0:T(8,128)(2,1)S(1)} %reshape.68.tiles), custom_call_target="tpu_custom_call" | custom-call | flops 100000 | bytes 1000000 | tf_op jit(solution)/shard_map/pack_step/pallas_call | solution.py:194
  5.0 22.8 %all_to_all.10.w0 = bf16[8,400,128]{2,1,0:T(8,128)(2,1)S(1)} all-to-all(bf16[8,400,128]{2,1,0:T(8,128)(2,1)S(1)} %pack_step.1), channel_id=1, replica_groups=mesh['z'=16,'x'=4,'y'=8,'core'=2] {'y'}, dimensions={0} | all-to-all | bytes 1638400 | tf_op jit(solution)/shard_map/all_to_all | solution.py:265
  27.8 12.0 %collective-permute-start = (bf16[8,400,128]{2,1,0:T(8,128)(2,1)S(1)}, bf16[8,400,128]{2,1,0:T(8,128)(2,1)S(1)}, u32[]{:S(2)}, u32[]{:S(2)}) collective-permute-start(bf16[8,400,128]{2,1,0:T(8,128)(2,1)S(1)} %all_to_all.10.w0), channel_id=1, source_target_pairs={{0,1},{1,0},{2,3},{3,2},{4,5},{5,4},{6,7},{7,6},{8,9},{9,8},{10,11... | collective-permute-start | bytes 2457608 | tf_op jit(solution)/shard_map/ppermute | solution.py:277
  39.9 0.0 copy-done.2
  39.9 39.2 %all_gather.3 = bf16[16,12,16,128]{3,2,1,0:T(8,128)(2,1)S(1)} all-gather(bf16[1,12,16,128]{3,2,1,0:T(8,128)(2,1)S(1)} %bitcast.16), channel_id=1, replica_groups=mesh['z'=16,'x'=4,'y'=8,'core'=2] {'z'}, dimensions={0}, use_global_device_ids=true | all-gather | bytes 835584 | tf_op jit(solution)/shard_map/all_gather | solution.py:268
  79.0 1.0 fusion
  80.1 3.1 %collective-permute-start.1 = (bf16[1536,128]{1,0:T(8,128)(2,1)}, bf16[1536,128]{1,0:T(8,128)(2,1)S(1)}, u32[]{:S(2)}, u32[]{:S(2)}) collective-permute-start(bf16[1536,128]{1,0:T(8,128)(2,1)} %bitcast.5), channel_id=1, source_target_pairs={{0,16},{16,0},{32,48},{48,32},{1,17},{17,1},{33,49},{49,33},{2,18}... | collective-permute-start | bytes 1179656 | tf_op jit(solution)/shard_map/ppermute | solution.py:271
  83.2 3.7 %collective-permute-start.4 = (bf16[1536,128]{1,0:T(8,128)(2,1)}, bf16[1536,128]{1,0:T(8,128)(2,1)S(1)}, u32[]{:S(2)}, u32[]{:S(2)}) collective-permute-start(bf16[1536,128]{1,0:T(8,128)(2,1)} %bitcast.6), channel_id=1, source_target_pairs={{0,48},{16,32},{32,16},{48,0},{1,49},{17,33},{33,17},{49,1},{2,50}... | collective-permute-start | bytes 1179656 | tf_op jit(solution)/shard_map/ppermute | solution.py:272
  86.9 2.8 %collective-permute-start.3 = (bf16[1536,128]{1,0:T(8,128)(2,1)}, bf16[1536,128]{1,0:T(8,128)(2,1)}, u32[]{:S(2)}, u32[]{:S(2)}) collective-permute-start(bf16[1536,128]{1,0:T(8,128)(2,1)} %bitcast.5), channel_id=1, source_target_pairs={{0,48},{16,32},{32,16},{48,0},{1,49},{17,33},{33,17},{49,1},{2,50}... | collective-permute-start | bytes 1179656 | tf_op jit(solution)/shard_map/ppermute | solution.py:274
  89.7 1.9 %collective-permute-start.2 = (bf16[1536,128]{1,0:T(8,128)(2,1)}, bf16[1536,128]{1,0:T(8,128)(2,1)}, u32[]{:S(2)}, u32[]{:S(2)}) collective-permute-start(bf16[1536,128]{1,0:T(8,128)(2,1)} %bitcast.6), channel_id=1, source_target_pairs={{0,16},{16,0},{32,48},{48,32},{1,17},{17,1},{33,49},{49,33},{2,18}... | collective-permute-start | bytes 1179656 | tf_op jit(solution)/shard_map/ppermute | solution.py:273
  91.6 0.0 collective-permute-done.1.x1a
  91.6 3.7 %collective-permute-start.5 = (bf16[1536,128]{1,0:T(8,128)(2,1)S(1)}, bf16[1536,128]{1,0:T(8,128)(2,1)S(1)}, u32[]{:S(2)}, u32[]{:S(2)}) collective-permute-start(bf16[1536,128]{1,0:T(8,128)(2,1)S(1)} %collective-permute-done.1.x1a), channel_id=1, source_target_pairs={{0,48},{16,32},{32,16},{48,0},{1,49},{17,33},{33,17},{49,1},{2,50}... | collective-permute-start | bytes 1179656 | tf_op jit(solution)/shard_map/ppermute | solution.py:275
  95.4 0.0 collective-permute-done.4.x3b
  95.4 2.8 %collective-permute-start.6 = (bf16[1536,128]{1,0:T(8,128)(2,1)S(1)}, bf16[1536,128]{1,0:T(8,128)(2,1)S(1)}, u32[]{:S(2)}, u32[]{:S(2)}) collective-permute-start(bf16[1536,128]{1,0:T(8,128)(2,1)S(1)} %collective-permute-done.4.x3b), channel_id=1, source_target_pairs={{0,16},{16,0},{32,48},{48,32},{1,17},{17,1},{33,49},{49,33},{2,18}... | collective-permute-start | bytes 1179656 | tf_op jit(solution)/shard_map/ppermute | solution.py:276
  98.2 0.0 collective-permute-done.w1
  98.2 0.2 collective-permute-done.3.x3a
  98.4 2.3 %collective-permute-done.2.x1b = bf16[1536,128]{1,0:T(8,128)(2,1)} collective-permute-done((bf16[1536,128]{1,0:T(8,128)(2,1)}, bf16[1536,128]{1,0:T(8,128)(2,1)}, u32[]{:S(2)}, u32[]{:S(2)}) %collective-permute-start.2) | collective-permute-done | bytes 393248 | tf_op jit(solution)/shard_map/ppermute | solution.py:273
  100.7 0.0 copy-start
  100.7 5.1 %early_step.1 = (bf16[12288,128]{1,0:T(8,128)(2,1)S(1)}, bf16[16,400,128]{2,1,0:T(8,128)(2,1)S(1)}, f32[448,128]{1,0:T(8,128)S(1)}, s32[3,256]{1,0:T(4,128)S(1)}) custom-call(s32[16,128]{1,0:T(8,128)S(1)} %maximum_convert_fusion.table, s32[1]{0:T(128)} %bitcast.1.here, bf16[3072,128]{1,0:T(8,128)(2,1)S(1)} %bitcast.13, ...), custom_call_target="tpu_custom_call" | custom-call | flops 1000000000 | bytes 8000000 | tf_op jit(solution)/shard_map/early_step/pallas_call | solution.py:207
  105.8 1.1 collective-permute-done.5.x2a
  106.9 0.6 collective-permute-done.6.x2b
  107.5 0.0 copy-done
  107.5 4.8 %main_step.1 = (bf16[128,384]{1,0:T(8,128)(2,1)}, bf16[384,128]{1,0:T(8,128)(2,1)S(1)}, bf16[12288,128]{1,0:T(8,128)(2,1)S(1)}, bf16[8,384,128]{2,1,0:T(8,128)(2,1)S(1)}) custom-call(s32[16,128]{1,0:T(8,128)S(1)} %maximum_convert_fusion.table, s32[1]{0:T(128)} %bitcast.1.here, s32[3,256]{1,0:T(4,128)S(1)} %get-tuple-element.10.todo, ...), custom_call_target="tpu_custom_call", output_to_operand_aliasing={{2}: (3, {})} | custom-call | flops 1000000000 | bytes 8000000 | tf_op jit(solution)/shard_map/main_step/pallas_call | solution.py:225
  112.4 10.3 %collective-permute-start.7 = (bf16[8,384,128]{2,1,0:T(8,128)(2,1)S(1)}, bf16[8,384,128]{2,1,0:T(8,128)(2,1)S(1)}, u32[]{:S(2)}, u32[]{:S(2)}) collective-permute-start(bf16[8,384,128]{2,1,0:T(8,128)(2,1)S(1)} %get-tuple-element.17), channel_id=1, source_target_pairs={{0,1},{1,0},{2,3},{3,2},{4,5},{5,4},{6,7},{7,6},{8,9},{9,8},{10,11... | collective-permute-start | bytes 2359304 | tf_op jit(solution)/shard_map/ppermute | solution.py:285
  122.7 2.0 %rest_step.1 = bf16[8,384,128]{2,1,0:T(8,128)(2,1)S(1)} custom-call(s32[16,128]{1,0:T(8,128)S(1)} %maximum_convert_fusion.table, bf16[12288,128]{1,0:T(8,128)(2,1)S(1)} %get-tuple-element.15.x, bf16[384,128]{1,0:T(8,128)(2,1)S(1)} %get-tuple-element.16.grad_t), custom_call_target="tpu_custom_call" | custom-call | flops 1000000000 | bytes 4000000 | tf_op jit(solution)/shard_map/rest_step/pallas_call | solution.py:244
  124.7 0.0 collective-permute-done.7
  124.7 1.1 add_convert_fusion
  125.8 3.5 %all-to-all-start.1 = ((bf16[8,384,128]{2,1,0:T(8,128)(2,1)}), bf16[8,384,128]{2,1,0:T(8,128)(2,1)S(1)}, u32[]{:S(2)}, u32[]{:S(2)}) async-start(bf16[8,384,128]{2,1,0:T(8,128)(2,1)} %add_convert_fusion), calls=%async_computation.1 | async-start | bytes 1572864 | tf_op jit(solution)/shard_map/all_to_all | solution.py:288
  129.3 23.5 %all-to-all-done.1 = bf16[8,384,128]{2,1,0:T(8,128)(2,1)S(1)} async-done(((bf16[8,384,128]{2,1,0:T(8,128)(2,1)}), bf16[8,384,128]{2,1,0:T(8,128)(2,1)S(1)}, u32[]{:S(2)}, u32[]{:S(2)}) %all-to-all-start.1) | async-done | bytes 786464 | tf_op jit(solution)/shard_map/all_to_all | solution.py:288
  152.9 0.1 convert_reduce_fusion
  153.0 0.1 reshape.73
  153.1 0.2 copy.9
  153.3 0.2 reshape.74
  153.5 0.7 select_convert_fusion
  (4 shorter events, 0.0 us)
Async XLA Ops:
  0.6 39.2 %copy-start.2 = (bf16[128,192]{0,1:T(8,128)(2,1)S(1)}, bf16[128,192]{0,1:T(8,128)(2,1)}, u32[]{:S(2)}) copy-start(bf16[128,192]{0,1:T(8,128)(2,1)} %param.5) | copy-start | bytes 147460
  2.4 0.7 copy-start.1
  27.8 70.3 %collective-permute-start = (bf16[8,400,128]{2,1,0:T(8,128)(2,1)S(1)}, bf16[8,400,128]{2,1,0:T(8,128)(2,1)S(1)}, u32[]{:S(2)}, u32[]{:S(2)}) collective-permute-start(bf16[8,400,128]{2,1,0:T(8,128)(2,1)S(1)} %all_to_all.10.w0), channel_id=1, source_target_pairs={{0,1},{1,0},{2,3},{3,2},{4,5},{5,4},{6,7},{7,6},{8,9},{9,8},{10,11... | collective-permute-start | bytes 2457608 | tf_op jit(solution)/shard_map/ppermute | solution.py:277
  80.1 11.6 %collective-permute-start.1 = (bf16[1536,128]{1,0:T(8,128)(2,1)}, bf16[1536,128]{1,0:T(8,128)(2,1)S(1)}, u32[]{:S(2)}, u32[]{:S(2)}) collective-permute-start(bf16[1536,128]{1,0:T(8,128)(2,1)} %bitcast.5), channel_id=1, source_target_pairs={{0,16},{16,0},{32,48},{48,32},{1,17},{17,1},{33,49},{49,33},{2,18}... | collective-permute-start | bytes 1179656 | tf_op jit(solution)/shard_map/ppermute | solution.py:271
  83.2 12.2 %collective-permute-start.4 = (bf16[1536,128]{1,0:T(8,128)(2,1)}, bf16[1536,128]{1,0:T(8,128)(2,1)S(1)}, u32[]{:S(2)}, u32[]{:S(2)}) collective-permute-start(bf16[1536,128]{1,0:T(8,128)(2,1)} %bitcast.6), channel_id=1, source_target_pairs={{0,48},{16,32},{32,16},{48,0},{1,49},{17,33},{33,17},{49,1},{2,50}... | collective-permute-start | bytes 1179656 | tf_op jit(solution)/shard_map/ppermute | solution.py:272
  86.9 11.5 %collective-permute-start.3 = (bf16[1536,128]{1,0:T(8,128)(2,1)}, bf16[1536,128]{1,0:T(8,128)(2,1)}, u32[]{:S(2)}, u32[]{:S(2)}) collective-permute-start(bf16[1536,128]{1,0:T(8,128)(2,1)} %bitcast.5), channel_id=1, source_target_pairs={{0,48},{16,32},{32,16},{48,0},{1,49},{17,33},{33,17},{49,1},{2,50}... | collective-permute-start | bytes 1179656 | tf_op jit(solution)/shard_map/ppermute | solution.py:274
  89.7 11.0 %collective-permute-start.2 = (bf16[1536,128]{1,0:T(8,128)(2,1)}, bf16[1536,128]{1,0:T(8,128)(2,1)}, u32[]{:S(2)}, u32[]{:S(2)}) collective-permute-start(bf16[1536,128]{1,0:T(8,128)(2,1)} %bitcast.6), channel_id=1, source_target_pairs={{0,16},{16,0},{32,48},{48,32},{1,17},{17,1},{33,49},{49,33},{2,18}... | collective-permute-start | bytes 1179656 | tf_op jit(solution)/shard_map/ppermute | solution.py:273
  91.6 15.3 %collective-permute-start.5 = (bf16[1536,128]{1,0:T(8,128)(2,1)S(1)}, bf16[1536,128]{1,0:T(8,128)(2,1)S(1)}, u32[]{:S(2)}, u32[]{:S(2)}) collective-permute-start(bf16[1536,128]{1,0:T(8,128)(2,1)S(1)} %collective-permute-done.1.x1a), channel_id=1, source_target_pairs={{0,48},{16,32},{32,16},{48,0},{1,49},{17,33},{33,17},{49,1},{2,50}... | collective-permute-start | bytes 1179656 | tf_op jit(solution)/shard_map/ppermute | solution.py:275
  95.4 12.2 %collective-permute-start.6 = (bf16[1536,128]{1,0:T(8,128)(2,1)S(1)}, bf16[1536,128]{1,0:T(8,128)(2,1)S(1)}, u32[]{:S(2)}, u32[]{:S(2)}) collective-permute-start(bf16[1536,128]{1,0:T(8,128)(2,1)S(1)} %collective-permute-done.4.x3b), channel_id=1, source_target_pairs={{0,16},{16,0},{32,48},{48,32},{1,17},{17,1},{33,49},{49,33},{2,18}... | collective-permute-start | bytes 1179656 | tf_op jit(solution)/shard_map/ppermute | solution.py:276
  100.7 6.9 %copy-start = (bf16[128,384]{1,0:T(8,128)(2,1)S(1)}, bf16[128,384]{1,0:T(8,128)(2,1)}, u32[]{:S(2)}) copy-start(bf16[128,384]{1,0:T(8,128)(2,1)} %up.1) | copy-start | bytes 294916
  112.4 12.3 %collective-permute-start.7 = (bf16[8,384,128]{2,1,0:T(8,128)(2,1)S(1)}, bf16[8,384,128]{2,1,0:T(8,128)(2,1)S(1)}, u32[]{:S(2)}, u32[]{:S(2)}) collective-permute-start(bf16[8,384,128]{2,1,0:T(8,128)(2,1)S(1)} %get-tuple-element.17), channel_id=1, source_target_pairs={{0,1},{1,0},{2,3},{3,2},{4,5},{5,4},{6,7},{7,6},{8,9},{9,8},{10,11... | collective-permute-start | bytes 2359304 | tf_op jit(solution)/shard_map/ppermute | solution.py:285
  125.8 27.1 %all-to-all-start.1 = ((bf16[8,384,128]{2,1,0:T(8,128)(2,1)}), bf16[8,384,128]{2,1,0:T(8,128)(2,1)S(1)}, u32[]{:S(2)}, u32[]{:S(2)}) async-start(bf16[8,384,128]{2,1,0:T(8,128)(2,1)} %add_convert_fusion), calls=%async_computation.1 | async-start | bytes 1572864 | tf_op jit(solution)/shard_map/all_to_all | solution.py:288

commit v4 on v2

--- a/solution.py
+++ b/solution.py
@@ -44,14 +44,14 @@
     return jnp.concatenate([ref[aligned(start0 * TILE, TILE), :], ref[aligned(start1 * TILE, TILE), :]], axis=0)
 
 
-def slot_grads(table, b, x, grad_t, dw, y):
+def slot_grads(table, x, grad_t, dw, b):
     low = lanes_below()
     for m in range(PAIRS):
         s = 2 * m
         cols = two(grad_t, table[b, F_LANE + s], table[b, F_LANE + s + 1])
         rows = two(x, table[b, s], table[b, s + 1])
         prod = lax.dot_general(cols, rows, (((1,), (1,)), ((), ())), preferred_element_type=jnp.float32)
-        dw[y, m * TILE : (m + 1) * TILE, :] = jnp.where(low, prod[:TILE], prod[TILE:]).astype(jnp.bfloat16)
+        dw[b, m * TILE : (m + 1) * TILE, :] = jnp.where(low, prod[:TILE], prod[TILE:]).astype(jnp.bfloat16)
 
 
 def lane_masks():
@@ -59,28 +59,7 @@
     return jnp.where(low, 1.0, 0.0).astype(jnp.bfloat16), jnp.where(low, 0.0, 1.0).astype(jnp.bfloat16)
 
 
-def early_kernel(table, here, x0, x1a, x1b, x3a, x3b, w0, w1, x, tiles, acc, todo, sem):
-    opposite = here[0] ^ 2
-    x[pl.ds(pl.multiple_of(opposite * COL_ROWS, COL_ROWS), COL_ROWS), :] = jnp.zeros((COL_ROWS, TOK), jnp.bfloat16)
-
-    def part(distance, start, size):
-        column = here[0] ^ distance
-        return x.at[pl.ds(pl.multiple_of(column * COL_ROWS + start, CUT), size), :]
-
-    moves = [
-        (x0, part(0, 0, COL_ROWS)),
-        (x1a, part(1, 0, CUT)),
-        (x1b, part(1, CUT, CUT)),
-        (x3a, part(3, 0, CUT)),
-        (x3b, part(3, CUT, CUT)),
-        (w0, tiles.at[0:NY]),
-        (w1, tiles.at[NY : 2 * NY]),
-    ]
-    copies = [pltpu.make_async_copy(a, b, sem.at[i]) for i, (a, b) in enumerate(moves)]
-    for c in copies:
-        c.start()
-    acc[...] = jnp.zeros_like(acc)
-
+def list_slots(table, opposite, todo):
     def sort_out(b, n):
         for s in range(CAP):
             todo[0, n] = b * 16 + s
@@ -89,14 +68,15 @@
             n = n + jnp.where((ahead >= 0) & (ahead < UNITS), 1, 0)
         return n
 
-    count = lax.fori_loop(0, 2 * NY, sort_out, 0)
+    count = lax.fori_loop(0, NY, sort_out, 0)
     for i in range(GROUP):
         todo[0, count + i] = 0
         todo[1, count + i] = PER_COL
     todo[2, 0] = count
+
+
+def add_blocks(table, tiles, x, acc):
     first, second = lane_masks()
-    for c in copies:
-        c.wait()
 
     def forward(b, carry):
         for m in range(PAIRS):
@@ -111,21 +91,11 @@
                 acc[aligned(table[b, F_LANE + s + p] * TILE, TILE), :] += prod[p * TILE : (p + 1) * TILE]
         return carry
 
-    lax.fori_loop(0, 2 * NY, forward, 0, unroll=2)
-
-
-def main_kernel(table, here, todo, x_in, tiles, acc_in, x2a, x2b, up, out, grad_t, x, dw, acc, sem):
-    base = (here[0] ^ 2) * COL_ROWS
-    copies = [
-        pltpu.make_async_copy(x2a, x.at[pl.ds(pl.multiple_of(base, CUT), CUT), :], sem.at[0]),
-        pltpu.make_async_copy(x2b, x.at[pl.ds(pl.multiple_of(base + CUT, CUT), CUT), :], sem.at[1]),
-    ]
-    for c in copies:
-        c.start()
-    acc[...] = acc_in[...]
+    lax.fori_loop(0, NY, forward, 0, unroll=4)
+
+
+def add_listed(todo, table, tiles, x, acc):
     first, second = lane_masks()
-    for c in copies:
-        c.wait()
 
     def forward(g, carry):
         for i in range(GROUP):
@@ -142,6 +112,58 @@
         return carry
 
     lax.fori_loop(0, (todo[2, 0] + GROUP - 1) // GROUP, forward, 0)
+
+
+def own_kernel(table, here, x0, x1a, x1b, x3a, x3b, w, x, tiles, acc, todo, sem):
+    opposite = here[0] ^ 2
+    x[pl.ds(pl.multiple_of(opposite * COL_ROWS, COL_ROWS), COL_ROWS), :] = jnp.zeros((COL_ROWS, TOK), jnp.bfloat16)
+
+    def part(distance, start, size):
+        column = here[0] ^ distance
+        return x.at[pl.ds(pl.multiple_of(column * COL_ROWS + start, CUT), size), :]
+
+    moves = [
+        (x0, part(0, 0, COL_ROWS)),
+        (x1a, part(1, 0, CUT)),
+        (x1b, part(1, CUT, CUT)),
+        (x3a, part(3, 0, CUT)),
+        (x3b, part(3, CUT, CUT)),
+        (w, tiles),
+    ]
+    copies = [pltpu.make_async_copy(a, b, sem.at[i]) for i, (a, b) in enumerate(moves)]
+    for c in copies:
+        c.start()
+    acc[...] = jnp.zeros_like(acc)
+    list_slots(table, opposite, todo)
+    for c in copies:
+        c.wait()
+    add_blocks(table, tiles, x, acc)
+
+
+def other_kernel(table, here, x, acc_in, w, tiles, acc, todo, sem):
+    copy = pltpu.make_async_copy(w, tiles, sem.at[0])
+    copy.start()
+    acc[...] = acc_in[...]
+    list_slots(table, here[0] ^ 2, todo)
+    copy.wait()
+    add_blocks(table, tiles, x, acc)
+
+
+def main_kernel(
+    table0, table1, here, todo0, todo1, x_in, tiles0, tiles1, acc_in, x2a, x2b, up, out, grad_t, x, dw, acc, sem
+):
+    base = (here[0] ^ 2) * COL_ROWS
+    copies = [
+        pltpu.make_async_copy(x2a, x.at[pl.ds(pl.multiple_of(base, CUT), CUT), :], sem.at[0]),
+        pltpu.make_async_copy(x2b, x.at[pl.ds(pl.multiple_of(base + CUT, CUT), CUT), :], sem.at[1]),
+    ]
+    for c in copies:
+        c.start()
+    acc[...] = acc_in[...]
+    for c in copies:
+        c.wait()
+    add_listed(todo0, table0, tiles0, x, acc)
+    add_listed(todo1, table1, tiles1, x, acc)
     pre = acc[:FF_LOC].T
     cumul = 0.5 * (1.0 + lax.erf(pre * 0.7071067811865476))
     density = jnp.exp(-0.5 * pre * pre) * 0.3989422804014327
@@ -149,59 +171,73 @@
     grad_t[...] = (up[...].astype(jnp.float32) * (cumul + pre * density)).T.astype(jnp.bfloat16)
 
     def backward(y, carry):
-        slot_grads(table, NY + y, x, grad_t, dw, y)
+        slot_grads(table1, x, grad_t, dw, y)
         return carry
 
-    lax.fori_loop(0, NY, backward, 0, unroll=2)
+    lax.fori_loop(0, NY, backward, 0, unroll=4)
 
 
 def rest_kernel(table, x, grad_t, dw):
     def backward(y, carry):
-        slot_grads(table, y, x, grad_t, dw, y)
+        slot_grads(table, x, grad_t, dw, y)
         return carry
 
-    lax.fori_loop(0, NY, backward, 0, unroll=2)
+    lax.fori_loop(0, NY, backward, 0, unroll=4)
 
 
 def params(mib):
     return pltpu.CompilerParams(vmem_limit_bytes=mib << 20)
 
 
-def early_step(table, here, *parts):
+X_SHAPE = jax.ShapeDtypeStruct((X_ROWS, TOK), jnp.bfloat16)
+TILES_SHAPE = jax.ShapeDtypeStruct((NY, ROWS, PAIR), jnp.bfloat16)
+ACC_SHAPE = jax.ShapeDtypeStruct((FF_LOC + TILE, TOK), jnp.float32)
+TODO_SHAPE = jax.ShapeDtypeStruct((3, 128), jnp.int32)
+
+
+def own_step(table, here, *parts):
     return pl.pallas_call(
-        early_kernel,
-        out_shape=(
-            jax.ShapeDtypeStruct((X_ROWS, TOK), jnp.bfloat16),
-            jax.ShapeDtypeStruct((2 * NY, ROWS, PAIR), jnp.bfloat16),
-            jax.ShapeDtypeStruct((FF_LOC + TILE, TOK), jnp.float32),
-            jax.ShapeDtypeStruct((3, 256), jnp.int32),
-        ),
-        in_specs=[SMEM, SMEM] + [ANY] * 7,
+        own_kernel,
+        out_shape=(X_SHAPE, TILES_SHAPE, ACC_SHAPE, TODO_SHAPE),
+        in_specs=[SMEM, SMEM] + [ANY] * 6,
         out_specs=(VMEM, VMEM, VMEM, SMEM),
-        scratch_shapes=[pltpu.SemaphoreType.DMA((7,))],
+        scratch_shapes=[pltpu.SemaphoreType.DMA((6,))],
         compiler_params=params(12),
-        cost_estimate=pl.CostEstimate(flops=10**9, bytes_accessed=8 * 10**6, transcendentals=0),
-        name="early_step",
+        cost_estimate=pl.CostEstimate(flops=5 * 10**8, bytes_accessed=6 * 10**6, transcendentals=0),
+        name="own_step",
     )(table, here, *parts)
 
 
-def main_step(table, here, todo, x, tiles, acc, x2a, x2b, up):
+def other_step(table, here, x, acc, w):
+    return pl.pallas_call(
+        other_kernel,
+        out_shape=(TILES_SHAPE, ACC_SHAPE, TODO_SHAPE),
+        in_specs=[SMEM, SMEM, VMEM, VMEM, ANY],
+        out_specs=(VMEM, VMEM, SMEM),
+        scratch_shapes=[pltpu.SemaphoreType.DMA((1,))],
+        compiler_params=params(12),
+        cost_estimate=pl.CostEstimate(flops=5 * 10**8, bytes_accessed=4 * 10**6, transcendentals=0),
+        name="other_step",
+    )(table, here, x, acc, w)
+
+
+def main_step(*operands):
     return pl.pallas_call(
         main_kernel,
         out_shape=(
             jax.ShapeDtypeStruct((TOK, FF_LOC), jnp.bfloat16),
             jax.ShapeDtypeStruct((FF_LOC, TOK), jnp.bfloat16),
-            jax.ShapeDtypeStruct((X_ROWS, TOK), jnp.bfloat16),
+            X_SHAPE,
             jax.ShapeDtypeStruct((NY, PACK, PAIR), jnp.bfloat16),
         ),
-        in_specs=[SMEM, SMEM, SMEM, VMEM, VMEM, VMEM, ANY, ANY, VMEM],
+        in_specs=[SMEM] * 5 + [VMEM] * 4 + [ANY, ANY, VMEM],
         out_specs=(VMEM, VMEM, VMEM, VMEM),
         scratch_shapes=[pltpu.VMEM((FF_LOC + TILE, TOK), jnp.float32), pltpu.SemaphoreType.DMA((2,))],
-        input_output_aliases={3: 2},
+        input_output_aliases={5: 2},
         compiler_params=params(14),
         cost_estimate=pl.CostEstimate(flops=10**9, bytes_accessed=8 * 10**6, transcendentals=10**5),
         name="main_step",
-    )(table, here, todo, x, tiles, acc, x2a, x2b, up)
+    )(*operands)
 
 
 def rest_step(table, x, grad_t):
@@ -250,14 +286,17 @@
     x2b = lax.ppermute(x3b, "x", near)
     w_other = lax.ppermute(w_own, "core", SWAP)
 
-    table = jnp.concatenate(
-        [jnp.sum(w[:, PACK:, :].astype(jnp.float32), axis=1) for w in (w_own, w_other)], axis=0
-    ).astype(jnp.int32)
+    table0, table1 = (
+        jnp.sum(w[:, PACK:, :].astype(jnp.float32), axis=1).astype(jnp.int32) for w in (w_own, w_other)
+    )
     here = lax.axis_index("x").astype(jnp.int32).reshape(1)
-    x, tiles, acc, todo = early_step(table, here, x0, x1a, x1b, x3a, x3b, w_own, w_other)
-    output, grad, x, theirs = main_step(table, here, todo, x, tiles, acc, x2a, x2b, upstream)
+    x, tiles0, acc, todo0 = own_step(table0, here, x0, x1a, x1b, x3a, x3b, w_own)
+    tiles1, acc, todo1 = other_step(table1, here, x, acc, w_other)
+    output, grad, x, theirs = main_step(
+        table0, table1, here, todo0, todo1, x, tiles0, tiles1, acc, x2a, x2b, upstream
+    )
     arrived = lax.ppermute(theirs, "core", SWAP)
-    mine = rest_step(table, x, grad)
+    mine = rest_step(table0, x, grad)
     both = (mine.astype(jnp.float32) + arrived.astype(jnp.float32)).astype(jnp.bfloat16)
     parts = lax.all_to_all(both, "y", split_axis=0, concat_axis=0, tiled=True)
     summed = jnp.sum(parts.astype(jnp.float32), axis=0)

time: 155 us -> 141 us (0.910)
  blocking collectives: 62 us -> 40.8 us
  waiting for transfers between devices: 27.2 us -> 32.9 us
    all_to_all x1 -> x0, blocking collectives: 22.8 us -> none  [body(): w_own = lax.all_to_all(wide, 'y', split_axis=0, concat_axis=0, tiled=True)]
    ppermute x1, starting transfers between devices: 10.9 us -> 3.07 us  [body(): arrived = lax.ppermute(theirs, 'core', SWAP)]
    all_to_all x0 -> x1, starting transfers between devices: none -> 7.64 us  [body(): w_own = lax.all_to_all(wide, 'y', split_axis=0, concat_axis=0, tiled=True)]
    ppermute x1, waiting for transfers between devices: 0.17 us -> 6.23 us  [body(): x3a = lax.ppermute(lower, 'x', far)]
    all_to_all x1, starting transfers between devices: 3.55 us -> 7.2 us  [body(): parts = lax.all_to_all(both, 'y', split_axis=0, concat_axis=0, tiled=True)]
    ppermute x1, starting transfers between devices: 12 us -> 8.71 us  [body(): w_other = lax.ppermute(w_own, 'core', SWAP)]
    ppermute x1, waiting for transfers between devices: 2.29 us -> 0.01 us  [body(): x1b = lax.ppermute(upper, 'x', near)]
    all_gather x1, blocking collectives: 39.2 us -> 40.8 us  [body(): x0 = lax.all_gather(x_mine, 'z', axis=0, tiled=True).reshape(COL_ROWS, TOK)]
  transfers between devices with their start and end apart: 9 -> 10, of which waited for: 5 -> 4; matrix products, arithmetic and copies ran while one was open for 1% -> 1% of each run, Pallas kernels for 5% -> 6%
where the time goes in v4:
time: 141 us; the launch traced here: 140 us
  starting transfers between devices  44.3 us (31%)
  blocking collectives  40.8 us (29%)
  waiting for transfers between devices  32.9 us (23%)
  Pallas kernels  13.9 us (10%)
  local copies, waits for them, and re-layouts  3.9 us (3%)
  other arithmetic  2.84 us (2%)
  between operations  1.53 us (1%)
    all_gather x1, blocking collectives, body(): x0 = lax.all_gather(x_mine, 'z', axis=0, tiled=True).reshape(COL_ROWS, TOK)  40.8 us
    all_to_all x1, waiting for transfers between devices, body(): parts = lax.all_to_all(both, 'y', split_axis=0, concat_axis=0, tiled=True)  23.6 us
    ppermute x1, starting transfers between devices, body(): w_other = lax.ppermute(w_own, 'core', SWAP)  8.71 us
    all_to_all x1, starting transfers between devices, body(): w_own = lax.all_to_all(wide, 'y', split_axis=0, concat_axis=0, tiled=True)  7.64 us
    all_to_all x1, starting transfers between devices, body(): parts = lax.all_to_all(both, 'y', split_axis=0, concat_axis=0, tiled=True)  7.2 us
    ppermute x1, waiting for transfers between devices, body(): x3a = lax.ppermute(lower, 'x', far)  6.23 us
    pallas_call x1, Pallas kernels, main_step(): pl.pallas_call(main_kernel, out_shape=(jax.ShapeDtypeStruct((TOK, FF_LOC)...  5.47 us
    ppermute x1, starting transfers between devices, body(): x2a = lax.ppermute(x1a, 'x', far)  4.28 us
  transfers between devices with their start and end apart: 10, of which 4 were waited for; matrix products, arithmetic and copies ran while one was open for 1% of the time, Pallas kernels for 6%

profile of v4, /device:TPU:1, one launch (start us, length us, event | category | flops | bytes accessed | tf_op | source)
XLA Modules:
  0.0 140.2 jit_solution(13996069361911752236)
XLA Ops:
  1.3 1.1 reshape.226
  2.4 0.1 select_bitcast_fusion
  2.5 0.1 copy.12
  2.7 0.0 copy-start.1
  2.7 0.1 reshape.227
  2.8 0.7 fusion.1
  3.5 0.1 add_convert_fusion.1
  3.6 1.0 broadcast_in_dim.34
  4.6 7.6 %all-to-all-start = ((bf16[8,400,128]{2,1,0:T(8,128)(2,1)}), bf16[8,400,128]{2,1,0:T(8,128)(2,1)S(1)}, u32[]{:S(2)}, u32[]{:S(2)}) async-start(bf16[8,400,128]{2,1,0:T(8,128)(2,1)} %broadcast_in_dim.34), calls=%async_computation | async-start | bytes 1638400 | tf_op jit(solution)/shard_map/all_to_all | solution.py:275
  12.3 0.0 copy-done.1
  12.3 40.8 %all_gather.3 = bf16[16,12,16,128]{3,2,1,0:T(8,128)(2,1)S(1)} all-gather(bf16[1,12,16,128]{3,2,1,0:T(8,128)(2,1)S(1)} %bitcast.32), channel_id=1, replica_groups=mesh['z'=16,'x'=4,'y'=8,'core'=2] {'z'}, dimensions={0}, use_global_device_ids=true | all-gather | bytes 835584 | tf_op jit(solution)/shard_map/all_gather | solution.py:278
  53.1 0.0 all-to-all-done.w
  53.1 8.7 %collective-permute-start = (bf16[8,400,128]{2,1,0:T(8,128)(2,1)S(1)}, bf16[8,400,128]{2,1,0:T(8,128)(2,1)S(1)}, u32[]{:S(2)}, u32[]{:S(2)}) collective-permute-start(bf16[8,400,128]{2,1,0:T(8,128)(2,1)S(1)} %all-to-all-done.w), channel_id=1, source_target_pairs={{0,1},{1,0},{2,3},{3,2},{4,5},{5,4},{6,7},{7,6},{8,9},{9,8},{10,11... | collective-permute-start | bytes 2457608 | tf_op jit(solution)/shard_map/ppermute | solution.py:287
  61.8 1.0 fusion.2
  62.8 3.0 %collective-permute-start.1 = (bf16[1536,128]{1,0:T(8,128)(2,1)}, bf16[1536,128]{1,0:T(8,128)(2,1)S(1)}, u32[]{:S(2)}, u32[]{:S(2)}) collective-permute-start(bf16[1536,128]{1,0:T(8,128)(2,1)} %bitcast.9), channel_id=1, source_target_pairs={{0,16},{16,0},{32,48},{48,32},{1,17},{17,1},{33,49},{49,33},{2,18}... | collective-permute-start | bytes 1179656 | tf_op jit(solution)/shard_map/ppermute | solution.py:281
  65.9 3.7 %collective-permute-start.4 = (bf16[1536,128]{1,0:T(8,128)(2,1)}, bf16[1536,128]{1,0:T(8,128)(2,1)S(1)}, u32[]{:S(2)}, u32[]{:S(2)}) collective-permute-start(bf16[1536,128]{1,0:T(8,128)(2,1)} %bitcast.10), channel_id=1, source_target_pairs={{0,48},{16,32},{32,16},{48,0},{1,49},{17,33},{33,17},{49,1},{2,50}... | collective-permute-start | bytes 1179656 | tf_op jit(solution)/shard_map/ppermute | solution.py:282
  69.6 2.8 %collective-permute-start.3 = (bf16[1536,128]{1,0:T(8,128)(2,1)}, bf16[1536,128]{1,0:T(8,128)(2,1)}, u32[]{:S(2)}, u32[]{:S(2)}) collective-permute-start(bf16[1536,128]{1,0:T(8,128)(2,1)} %bitcast.9), channel_id=1, source_target_pairs={{0,48},{16,32},{32,16},{48,0},{1,49},{17,33},{33,17},{49,1},{2,50}... | collective-permute-start | bytes 1179656 | tf_op jit(solution)/shard_map/ppermute | solution.py:284
  72.4 1.9 %collective-permute-start.2 = (bf16[1536,128]{1,0:T(8,128)(2,1)}, bf16[1536,128]{1,0:T(8,128)(2,1)}, u32[]{:S(2)}, u32[]{:S(2)}) collective-permute-start(bf16[1536,128]{1,0:T(8,128)(2,1)} %bitcast.10), channel_id=1, source_target_pairs={{0,16},{16,0},{32,48},{48,32},{1,17},{17,1},{33,49},{49,33},{2,18}... | collective-permute-start | bytes 1179656 | tf_op jit(solution)/shard_map/ppermute | solution.py:283
  74.3 1.3 collective-permute-done.1.x1a
  75.6 4.3 %collective-permute-start.5 = (bf16[1536,128]{1,0:T(8,128)(2,1)S(1)}, bf16[1536,128]{1,0:T(8,128)(2,1)}, u32[]{:S(2)}, u32[]{:S(2)}) collective-permute-start(bf16[1536,128]{1,0:T(8,128)(2,1)S(1)} %collective-permute-done.1.x1a), channel_id=1, source_target_pairs={{0,48},{16,32},{32,16},{48,0},{1,49},{17,33},{33,17},{49,1},{2,50}... | collective-permute-start | bytes 1179656 | tf_op jit(solution)/shard_map/ppermute | solution.py:285
  79.9 0.0 collective-permute-done.4.x3b
  79.9 1.9 %collective-permute-start.6 = (bf16[1536,128]{1,0:T(8,128)(2,1)S(1)}, bf16[1536,128]{1,0:T(8,128)(2,1)}, u32[]{:S(2)}, u32[]{:S(2)}) collective-permute-start(bf16[1536,128]{1,0:T(8,128)(2,1)S(1)} %collective-permute-done.4.x3b), channel_id=1, source_target_pairs={{0,16},{16,0},{32,48},{48,32},{1,17},{17,1},{33,49},{49,33},{2,18}... | collective-permute-start | bytes 1179656 | tf_op jit(solution)/shard_map/ppermute | solution.py:286
  81.9 6.2 %collective-permute-done.3.x3a = bf16[1536,128]{1,0:T(8,128)(2,1)} collective-permute-done((bf16[1536,128]{1,0:T(8,128)(2,1)}, bf16[1536,128]{1,0:T(8,128)(2,1)}, u32[]{:S(2)}, u32[]{:S(2)}) %collective-permute-start.3) | collective-permute-done | bytes 393248 | tf_op jit(solution)/shard_map/ppermute | solution.py:284
  88.1 0.0 collective-permute-done.2.x1b
  88.1 3.7 %own_step.1 = (bf16[12288,128]{1,0:T(8,128)(2,1)S(1)}, bf16[8,400,128]{2,1,0:T(8,128)(2,1)S(1)}, f32[448,128]{1,0:T(8,128)S(1)}, s32[3,128]{1,0:T(4,128)S(1)}) custom-call(s32[8,128]{1,0:T(8,128)S(1)} %convert_element_type.41.table.table0, s32[1]{0:T(128)} %bitcast.5.here, bf16[3072,128]{1,0:T(8,128)(2,1)S(1)} %bitcast.30, ...), custom_call_target="tpu_custom_call" | custom-call | flops 500000000 | bytes 6000000 | tf_op jit(solution)/shard_map/own_step/pallas_call | solution.py:199
  91.8 0.0 collective-permute-done.w
  91.8 0.0 copy-start
  91.8 2.9 %other_step.1 = (bf16[8,400,128]{2,1,0:T(8,128)(2,1)S(1)}, f32[448,128]{1,0:T(8,128)S(1)}, s32[3,128]{1,0:T(4,128)S(1)}) custom-call(s32[8,128]{1,0:T(8,128)S(1)} %convert_element_type.43.table.table1, s32[1]{0:T(128)} %bitcast.5.here, bf16[12288,128]{1,0:T(8,128)(2,1)S(1)} %get-tuple-element.14.x.x_in, f32[448,128]{1,0:T(8,128)S(1)} %get-tuple-element.15.acc_in, ...), custom_call_target="tpu_custom_call" | custom-call | flops 500000000 | bytes 4000000 | tf_op jit(solution)/shard_map/other_step/pallas_call | solution.py:212
  94.7 1.8 %collective-permute-done.5.x2a = bf16[1536,128]{1,0:T(8,128)(2,1)} collective-permute-done((bf16[1536,128]{1,0:T(8,128)(2,1)S(1)}, bf16[1536,128]{1,0:T(8,128)(2,1)}, u32[]{:S(2)}, u32[]{:S(2)}) %collective-permute-start.5) | collective-permute-done | bytes 393248 | tf_op jit(solution)/shard_map/ppermute | solution.py:285
  96.5 0.0 collective-permute-done.6.x2b
  96.5 0.0 copy-done
  96.5 5.5 %main_step.1 = (bf16[128,384]{1,0:T(8,128)(2,1)}, bf16[384,128]{1,0:T(8,128)(2,1)S(1)}, bf16[12288,128]{1,0:T(8,128)(2,1)S(1)}, bf16[8,384,128]{2,1,0:T(8,128)(2,1)S(1)}) custom-call(s32[8,128]{1,0:T(8,128)S(1)} %convert_element_type.41.table.table0, s32[8,128]{1,0:T(8,128)S(1)} %convert_element_type.43.table.table1, ...), custom_call_target="tpu_custom_call", output_to_operand_aliasing={{2}: (5, {})} | custom-call | flops 1000000000 | bytes 8000000 | tf_op jit(solution)/shard_map/main_step/pallas_call | solution.py:225
  102.0 3.1 %collective-permute-start.7 = (bf16[8,384,128]{2,1,0:T(8,128)(2,1)S(1)}, bf16[8,384,128]{2,1,0:T(8,128)(2,1)S(1)}, u32[]{:S(2)}, u32[]{:S(2)}) collective-permute-start(bf16[8,384,128]{2,1,0:T(8,128)(2,1)S(1)} %get-tuple-element.23), channel_id=1, source_target_pairs={{0,1},{1,0},{2,3},{3,2},{4,5},{5,4},{6,7},{7,6},{8,9},{9,8},{10,11... | collective-permute-start | bytes 2359304 | tf_op jit(solution)/shard_map/ppermute | solution.py:298
  105.1 1.9 %rest_step.1 = bf16[8,384,128]{2,1,0:T(8,128)(2,1)S(1)} custom-call(s32[8,128]{1,0:T(8,128)S(1)} %convert_element_type.41.table.table0, bf16[12288,128]{1,0:T(8,128)(2,1)S(1)} %get-tuple-element.21.x, bf16[384,128]{1,0:T(8,128)(2,1)S(1)} %get-tuple-element.22.grad_t), custom_call_target="tpu_custom_call" | custom-call | flops 1000000000 | bytes 4000000 | tf_op jit(solution)/shard_map/rest_step/pallas_call | solution.py:244
  107.0 0.0 collective-permute-done.7
  107.0 1.1 add_convert_fusion
  108.1 7.2 %all-to-all-start.1 = ((bf16[8,384,128]{2,1,0:T(8,128)(2,1)}), bf16[8,384,128]{2,1,0:T(8,128)(2,1)S(1)}, u32[]{:S(2)}, u32[]{:S(2)}) async-start(bf16[8,384,128]{2,1,0:T(8,128)(2,1)} %add_convert_fusion), calls=%async_computation.1 | async-start | bytes 1572864 | tf_op jit(solution)/shard_map/all_to_all | solution.py:301
  115.3 23.6 %all-to-all-done.1 = bf16[8,384,128]{2,1,0:T(8,128)(2,1)S(1)} async-done(((bf16[8,384,128]{2,1,0:T(8,128)(2,1)}), bf16[8,384,128]{2,1,0:T(8,128)(2,1)S(1)}, u32[]{:S(2)}, u32[]{:S(2)}) %all-to-all-start.1) | async-done | bytes 786464 | tf_op jit(solution)/shard_map/all_to_all | solution.py:301
  138.9 0.1 convert_reduce_fusion
  139.0 0.1 reshape.231
  139.1 0.2 copy.13
  139.3 0.2 reshape.232
  139.5 0.7 select_convert_fusion
  (7 shorter events, 0.1 us)
Async XLA Ops:
  2.7 9.6 %copy-start.1 = (bf16[128,192]{0,1:T(8,128)(2,1)S(1)}, bf16[128,192]{0,1:T(8,128)(2,1)}, u32[]{:S(2)}) copy-start(bf16[128,192]{0,1:T(8,128)(2,1)} %param.5) | copy-start | bytes 147460
  4.6 48.5 %all-to-all-start = ((bf16[8,400,128]{2,1,0:T(8,128)(2,1)}), bf16[8,400,128]{2,1,0:T(8,128)(2,1)S(1)}, u32[]{:S(2)}, u32[]{:S(2)}) async-start(bf16[8,400,128]{2,1,0:T(8,128)(2,1)} %broadcast_in_dim.34), calls=%async_computation | async-start | bytes 1638400 | tf_op jit(solution)/shard_map/all_to_all | solution.py:275
  53.1 38.7 %collective-permute-start = (bf16[8,400,128]{2,1,0:T(8,128)(2,1)S(1)}, bf16[8,400,128]{2,1,0:T(8,128)(2,1)S(1)}, u32[]{:S(2)}, u32[]{:S(2)}) collective-permute-start(bf16[8,400,128]{2,1,0:T(8,128)(2,1)S(1)} %all-to-all-done.w), channel_id=1, source_target_pairs={{0,1},{1,0},{2,3},{3,2},{4,5},{5,4},{6,7},{7,6},{8,9},{9,8},{10,11... | collective-permute-start | bytes 2457608 | tf_op jit(solution)/shard_map/ppermute | solution.py:287
  62.8 12.7 %collective-permute-start.1 = (bf16[1536,128]{1,0:T(8,128)(2,1)}, bf16[1536,128]{1,0:T(8,128)(2,1)S(1)}, u32[]{:S(2)}, u32[]{:S(2)}) collective-permute-start(bf16[1536,128]{1,0:T(8,128)(2,1)} %bitcast.9), channel_id=1, source_target_pairs={{0,16},{16,0},{32,48},{48,32},{1,17},{17,1},{33,49},{49,33},{2,18}... | collective-permute-start | bytes 1179656 | tf_op jit(solution)/shard_map/ppermute | solution.py:281
  65.9 14.0 %collective-permute-start.4 = (bf16[1536,128]{1,0:T(8,128)(2,1)}, bf16[1536,128]{1,0:T(8,128)(2,1)S(1)}, u32[]{:S(2)}, u32[]{:S(2)}) collective-permute-start(bf16[1536,128]{1,0:T(8,128)(2,1)} %bitcast.10), channel_id=1, source_target_pairs={{0,48},{16,32},{32,16},{48,0},{1,49},{17,33},{33,17},{49,1},{2,50}... | collective-permute-start | bytes 1179656 | tf_op jit(solution)/shard_map/ppermute | solution.py:282
  69.6 18.5 %collective-permute-start.3 = (bf16[1536,128]{1,0:T(8,128)(2,1)}, bf16[1536,128]{1,0:T(8,128)(2,1)}, u32[]{:S(2)}, u32[]{:S(2)}) collective-permute-start(bf16[1536,128]{1,0:T(8,128)(2,1)} %bitcast.9), channel_id=1, source_target_pairs={{0,48},{16,32},{32,16},{48,0},{1,49},{17,33},{33,17},{49,1},{2,50}... | collective-permute-start | bytes 1179656 | tf_op jit(solution)/shard_map/ppermute | solution.py:284
  72.4 15.7 %collective-permute-start.2 = (bf16[1536,128]{1,0:T(8,128)(2,1)}, bf16[1536,128]{1,0:T(8,128)(2,1)}, u32[]{:S(2)}, u32[]{:S(2)}) collective-permute-start(bf16[1536,128]{1,0:T(8,128)(2,1)} %bitcast.10), channel_id=1, source_target_pairs={{0,16},{16,0},{32,48},{48,32},{1,17},{17,1},{33,49},{49,33},{2,18}... | collective-permute-start | bytes 1179656 | tf_op jit(solution)/shard_map/ppermute | solution.py:283
  75.6 20.9 %collective-permute-start.5 = (bf16[1536,128]{1,0:T(8,128)(2,1)S(1)}, bf16[1536,128]{1,0:T(8,128)(2,1)}, u32[]{:S(2)}, u32[]{:S(2)}) collective-permute-start(bf16[1536,128]{1,0:T(8,128)(2,1)S(1)} %collective-permute-done.1.x1a), channel_id=1, source_target_pairs={{0,48},{16,32},{32,16},{48,0},{1,49},{17,33},{33,17},{49,1},{2,50}... | collective-permute-start | bytes 1179656 | tf_op jit(solution)/shard_map/ppermute | solution.py:285
  79.9 16.6 %collective-permute-start.6 = (bf16[1536,128]{1,0:T(8,128)(2,1)S(1)}, bf16[1536,128]{1,0:T(8,128)(2,1)}, u32[]{:S(2)}, u32[]{:S(2)}) collective-permute-start(bf16[1536,128]{1,0:T(8,128)(2,1)S(1)} %collective-permute-done.4.x3b), channel_id=1, source_target_pairs={{0,16},{16,0},{32,48},{48,32},{1,17},{17,1},{33,49},{49,33},{2,18}... | collective-permute-start | bytes 1179656 | tf_op jit(solution)/shard_map/ppermute | solution.py:286
  91.8 4.7 %copy-start = (bf16[128,384]{1,0:T(8,128)(2,1)S(1)}, bf16[128,384]{1,0:T(8,128)(2,1)}, u32[]{:S(2)}) copy-start(bf16[128,384]{1,0:T(8,128)(2,1)} %up.1) | copy-start | bytes 294916
  102.0 5.0 %collective-permute-start.7 = (bf16[8,384,128]{2,1,0:T(8,128)(2,1)S(1)}, bf16[8,384,128]{2,1,0:T(8,128)(2,1)S(1)}, u32[]{:S(2)}, u32[]{:S(2)}) collective-permute-start(bf16[8,384,128]{2,1,0:T(8,128)(2,1)S(1)} %get-tuple-element.23), channel_id=1, source_target_pairs={{0,1},{1,0},{2,3},{3,2},{4,5},{5,4},{6,7},{7,6},{8,9},{9,8},{10,11... | collective-permute-start | bytes 2359304 | tf_op jit(solution)/shard_map/ppermute | solution.py:298
  108.1 30.8 %all-to-all-start.1 = ((bf16[8,384,128]{2,1,0:T(8,128)(2,1)}), bf16[8,384,128]{2,1,0:T(8,128)(2,1)S(1)}, u32[]{:S(2)}, u32[]{:S(2)}) async-start(bf16[8,384,128]{2,1,0:T(8,128)(2,1)} %add_convert_fusion), calls=%async_computation.1 | async-start | bytes 1572864 | tf_op jit(solution)/shard_map/all_to_all | solution.py:301

commit v5 on v4

--- a/solution.py
+++ b/solution.py
@@ -140,17 +140,8 @@
     add_blocks(table, tiles, x, acc)
 
 
-def other_kernel(table, here, x, acc_in, w, tiles, acc, todo, sem):
-    copy = pltpu.make_async_copy(w, tiles, sem.at[0])
-    copy.start()
-    acc[...] = acc_in[...]
-    list_slots(table, here[0] ^ 2, todo)
-    copy.wait()
-    add_blocks(table, tiles, x, acc)
-
-
 def main_kernel(
-    table0, table1, here, todo0, todo1, x_in, tiles0, tiles1, acc_in, x2a, x2b, up, out, grad_t, x, dw, acc, sem
+    table0, table1, here, todo, x_in, tiles0, tiles1, acc_in, x2a, x2b, up, out, grad_t, x, dw, acc, sem
 ):
     base = (here[0] ^ 2) * COL_ROWS
     copies = [
@@ -162,8 +153,8 @@
     acc[...] = acc_in[...]
     for c in copies:
         c.wait()
-    add_listed(todo0, table0, tiles0, x, acc)
-    add_listed(todo1, table1, tiles1, x, acc)
+    add_blocks(table1, tiles1, x, acc)
+    add_listed(todo, table0, tiles0, x, acc)
     pre = acc[:FF_LOC].T
     cumul = 0.5 * (1.0 + lax.erf(pre * 0.7071067811865476))
     density = jnp.exp(-0.5 * pre * pre) * 0.3989422804014327
@@ -208,19 +199,6 @@
     )(table, here, *parts)
 
 
-def other_step(table, here, x, acc, w):
-    return pl.pallas_call(
-        other_kernel,
-        out_shape=(TILES_SHAPE, ACC_SHAPE, TODO_SHAPE),
-        in_specs=[SMEM, SMEM, VMEM, VMEM, ANY],
-        out_specs=(VMEM, VMEM, SMEM),
-        scratch_shapes=[pltpu.SemaphoreType.DMA((1,))],
-        compiler_params=params(12),
-        cost_estimate=pl.CostEstimate(flops=5 * 10**8, bytes_accessed=4 * 10**6, transcendentals=0),
-        name="other_step",
-    )(table, here, x, acc, w)
-
-
 def main_step(*operands):
     return pl.pallas_call(
         main_kernel,
@@ -230,10 +208,10 @@
             X_SHAPE,
             jax.ShapeDtypeStruct((NY, PACK, PAIR), jnp.bfloat16),
         ),
-        in_specs=[SMEM] * 5 + [VMEM] * 4 + [ANY, ANY, VMEM],
+        in_specs=[SMEM] * 4 + [VMEM] * 4 + [ANY, ANY, VMEM],
         out_specs=(VMEM, VMEM, VMEM, VMEM),
         scratch_shapes=[pltpu.VMEM((FF_LOC + TILE, TOK), jnp.float32), pltpu.SemaphoreType.DMA((2,))],
-        input_output_aliases={5: 2},
+        input_output_aliases={4: 2},
         compiler_params=params(14),
         cost_estimate=pl.CostEstimate(flops=10**9, bytes_accessed=8 * 10**6, transcendentals=10**5),
         name="main_step",
@@ -290,11 +268,8 @@
         jnp.sum(w[:, PACK:, :].astype(jnp.float32), axis=1).astype(jnp.int32) for w in (w_own, w_other)
     )
     here = lax.axis_index("x").astype(jnp.int32).reshape(1)
-    x, tiles0, acc, todo0 = own_step(table0, here, x0, x1a, x1b, x3a, x3b, w_own)
-    tiles1, acc, todo1 = other_step(table1, here, x, acc, w_other)
-    output, grad, x, theirs = main_step(
-        table0, table1, here, todo0, todo1, x, tiles0, tiles1, acc, x2a, x2b, upstream
-    )
+    x, tiles, acc, todo = own_step(table0, here, x0, x1a, x1b, x3a, x3b, w_own)
+    output, grad, x, theirs = main_step(table0, table1, here, todo, x, tiles, w_other, acc, x2a, x2b, upstream)
     arrived = lax.ppermute(theirs, "core", SWAP)
     mine = rest_step(table0, x, grad)
     both = (mine.astype(jnp.float32) + arrived.astype(jnp.float32)).astype(jnp.bfloat16)

time: 141 us -> 140 us (level)
  Pallas kernels: 13.9 us -> 10.4 us
  waiting for transfers between devices: 32.9 us -> 35.7 us
    pallas_call x1 -> x0, Pallas kernels: 2.85 us -> none  [other_step(): pl.pallas_call(other_kernel, out_shape=(TILES_SHAPE, ACC_SHAPE, TODO_SHAP...]
    ppermute x1, waiting for transfers between devices: 1.83 us -> 4.58 us  [body(): x2a = lax.ppermute(x1a, 'x', far)]
  transfers between devices with their start and end apart: 10 -> 10, of which waited for: 4 -> 4; matrix products, arithmetic and copies ran while one was open for 1% -> 1% of each run, Pallas kernels for 6% -> 4%
where the time goes in v5:
time: 140 us
  starting transfers between devices  44.5 us (32%)
  blocking collectives  40.8 us (29%)
  waiting for transfers between devices  35.7 us (26%)
  Pallas kernels  10.4 us (7%)
  local copies, waits for them, and re-layouts  3.94 us (3%)
  other arithmetic  2.85 us (2%)
  between operations  1.52 us (1%)
    all_gather x1, blocking collectives, body(): x0 = lax.all_gather(x_mine, 'z', axis=0, tiled=True).reshape(COL_ROWS, TOK)  40.8 us
    all_to_all x1, waiting for transfers between devices, body(): parts = lax.all_to_all(both, 'y', split_axis=0, concat_axis=0, tiled=True)  23.6 us
    ppermute x1, starting transfers between devices, body(): w_other = lax.ppermute(w_own, 'core', SWAP)  8.71 us
    all_to_all x1, starting transfers between devices, body(): w_own = lax.all_to_all(wide, 'y', split_axis=0, concat_axis=0, tiled=True)  7.64 us
    all_to_all x1, starting transfers between devices, body(): parts = lax.all_to_all(both, 'y', split_axis=0, concat_axis=0, tiled=True)  7.18 us
    ppermute x1, waiting for transfers between devices, body(): x3a = lax.ppermute(lower, 'x', far)  6.13 us
    pallas_call x1, Pallas kernels, main_step(): pl.pallas_call(main_kernel, out_shape=(jax.ShapeDtypeStruct((TOK, FF_LOC)...  4.74 us
    ppermute x1, waiting for transfers between devices, body(): x2a = lax.ppermute(x1a, 'x', far)  4.58 us
  transfers between devices with their start and end apart: 10, of which 4 were waited for; matrix products, arithmetic and copies ran while one was open for 1% of the time, Pallas kernels for 4%

profile of v5, /device:TPU:1, one launch (start us, length us, event | category | flops | bytes accessed | tf_op | source)
XLA Modules:
  0.0 139.7 jit_solution(7367529051769261922)
XLA Ops:
  1.3 1.1 reshape.226
  2.4 0.1 select_bitcast_fusion
  2.5 0.1 copy.12
  2.7 0.0 copy-start.1
  2.7 0.1 reshape.227
  2.8 0.7 fusion.1
  3.5 0.1 add_convert_fusion.1
  3.6 1.0 broadcast_in_dim.34
  4.6 7.6 %all-to-all-start = ((bf16[8,400,128]{2,1,0:T(8,128)(2,1)}), bf16[8,400,128]{2,1,0:T(8,128)(2,1)S(1)}, u32[]{:S(2)}, u32[]{:S(2)}) async-start(bf16[8,400,128]{2,1,0:T(8,128)(2,1)} %broadcast_in_dim.34), calls=%async_computation | async-start | bytes 1638400 | tf_op jit(solution)/shard_map/all_to_all | solution.py:253
  12.3 0.0 copy-done.1
  12.3 40.8 %all_gather.3 = bf16[16,12,16,128]{3,2,1,0:T(8,128)(2,1)S(1)} all-gather(bf16[1,12,16,128]{3,2,1,0:T(8,128)(2,1)S(1)} %bitcast.32), channel_id=1, replica_groups=mesh['z'=16,'x'=4,'y'=8,'core'=2] {'z'}, dimensions={0}, use_global_device_ids=true | all-gather | bytes 835584 | tf_op jit(solution)/shard_map/all_gather | solution.py:256
  53.1 0.0 all-to-all-done.w
  53.1 8.7 %collective-permute-start = (bf16[8,400,128]{2,1,0:T(8,128)(2,1)S(1)}, bf16[8,400,128]{2,1,0:T(8,128)(2,1)S(1)}, u32[]{:S(2)}, u32[]{:S(2)}) collective-permute-start(bf16[8,400,128]{2,1,0:T(8,128)(2,1)S(1)} %all-to-all-done.w), channel_id=1, source_target_pairs={{0,1},{1,0},{2,3},{3,2},{4,5},{5,4},{6,7},{7,6},{8,9},{9,8},{10,11... | collective-permute-start | bytes 2457608 | tf_op jit(solution)/shard_map/ppermute | solution.py:265
  61.8 1.0 fusion.2
  62.9 3.0 %collective-permute-start.1 = (bf16[1536,128]{1,0:T(8,128)(2,1)}, bf16[1536,128]{1,0:T(8,128)(2,1)}, u32[]{:S(2)}, u32[]{:S(2)}) collective-permute-start(bf16[1536,128]{1,0:T(8,128)(2,1)} %bitcast.9), channel_id=1, source_target_pairs={{0,16},{16,0},{32,48},{48,32},{1,17},{17,1},{33,49},{49,33},{2,18}... | collective-permute-start | bytes 1179656 | tf_op jit(solution)/shard_map/ppermute | solution.py:259
  65.9 3.7 %collective-permute-start.4 = (bf16[1536,128]{1,0:T(8,128)(2,1)}, bf16[1536,128]{1,0:T(8,128)(2,1)}, u32[]{:S(2)}, u32[]{:S(2)}) collective-permute-start(bf16[1536,128]{1,0:T(8,128)(2,1)} %bitcast.10), channel_id=1, source_target_pairs={{0,48},{16,32},{32,16},{48,0},{1,49},{17,33},{33,17},{49,1},{2,50}... | collective-permute-start | bytes 1179656 | tf_op jit(solution)/shard_map/ppermute | solution.py:260
  69.6 2.8 %collective-permute-start.3 = (bf16[1536,128]{1,0:T(8,128)(2,1)}, bf16[1536,128]{1,0:T(8,128)(2,1)}, u32[]{:S(2)}, u32[]{:S(2)}) collective-permute-start(bf16[1536,128]{1,0:T(8,128)(2,1)} %bitcast.9), channel_id=1, source_target_pairs={{0,48},{16,32},{32,16},{48,0},{1,49},{17,33},{33,17},{49,1},{2,50}... | collective-permute-start | bytes 1179656 | tf_op jit(solution)/shard_map/ppermute | solution.py:262
  72.4 1.9 %collective-permute-start.2 = (bf16[1536,128]{1,0:T(8,128)(2,1)}, bf16[1536,128]{1,0:T(8,128)(2,1)}, u32[]{:S(2)}, u32[]{:S(2)}) collective-permute-start(bf16[1536,128]{1,0:T(8,128)(2,1)} %bitcast.10), channel_id=1, source_target_pairs={{0,16},{16,0},{32,48},{48,32},{1,17},{17,1},{33,49},{49,33},{2,18}... | collective-permute-start | bytes 1179656 | tf_op jit(solution)/shard_map/ppermute | solution.py:261
  74.3 1.4 collective-permute-done.1.x1a
  75.7 4.3 %collective-permute-start.5 = (bf16[1536,128]{1,0:T(8,128)(2,1)}, bf16[1536,128]{1,0:T(8,128)(2,1)S(1)}, u32[]{:S(2)}, u32[]{:S(2)}) collective-permute-start(bf16[1536,128]{1,0:T(8,128)(2,1)} %collective-permute-done.1.x1a), channel_id=1, source_target_pairs={{0,48},{16,32},{32,16},{48,0},{1,49},{17,33},{33,17},{49,1},{2,50}... | collective-permute-start | bytes 1179656 | tf_op jit(solution)/shard_map/ppermute | solution.py:263
  80.0 0.0 collective-permute-done.4.x3b
  80.0 1.9 %collective-permute-start.6 = (bf16[1536,128]{1,0:T(8,128)(2,1)}, bf16[1536,128]{1,0:T(8,128)(2,1)S(1)}, u32[]{:S(2)}, u32[]{:S(2)}) collective-permute-start(bf16[1536,128]{1,0:T(8,128)(2,1)} %collective-permute-done.4.x3b), channel_id=1, source_target_pairs={{0,16},{16,0},{32,48},{48,32},{1,17},{17,1},{33,49},{49,33},{2,18}... | collective-permute-start | bytes 1179656 | tf_op jit(solution)/shard_map/ppermute | solution.py:264
  82.0 6.1 %collective-permute-done.3.x3a = bf16[1536,128]{1,0:T(8,128)(2,1)} collective-permute-done((bf16[1536,128]{1,0:T(8,128)(2,1)}, bf16[1536,128]{1,0:T(8,128)(2,1)}, u32[]{:S(2)}, u32[]{:S(2)}) %collective-permute-start.3) | collective-permute-done | bytes 393248 | tf_op jit(solution)/shard_map/ppermute | solution.py:262
  88.1 0.0 collective-permute-done.2.x1b
  88.1 0.0 copy-start
  88.1 3.7 %own_step.1 = (bf16[12288,128]{1,0:T(8,128)(2,1)S(1)}, bf16[8,400,128]{2,1,0:T(8,128)(2,1)S(1)}, f32[448,128]{1,0:T(8,128)S(1)}, s32[3,128]{1,0:T(4,128)S(1)}) custom-call(s32[8,128]{1,0:T(8,128)S(1)} %convert_element_type.41.table.table0, s32[1]{0:T(128)} %bitcast.5.here, bf16[3072,128]{1,0:T(8,128)(2,1)S(1)} %bitcast.30, ...), custom_call_target="tpu_custom_call" | custom-call | flops 500000000 | bytes 6000000 | tf_op jit(solution)/shard_map/own_step/pallas_call | solution.py:190
  91.8 0.0 collective-permute-done.tiles1
  91.9 4.6 %collective-permute-done.5.x2a = bf16[1536,128]{1,0:T(8,128)(2,1)S(1)} collective-permute-done((bf16[1536,128]{1,0:T(8,128)(2,1)}, bf16[1536,128]{1,0:T(8,128)(2,1)S(1)}, u32[]{:S(2)}, u32[]{:S(2)}) %collective-permute-start.5) | collective-permute-done | bytes 393248 | tf_op jit(solution)/shard_map/ppermute | solution.py:263
  96.5 0.0 collective-permute-done.6.x2b
  96.5 0.0 copy-done
  96.5 4.7 %main_step.1 = (bf16[128,384]{1,0:T(8,128)(2,1)}, bf16[384,128]{1,0:T(8,128)(2,1)S(1)}, bf16[12288,128]{1,0:T(8,128)(2,1)S(1)}, bf16[8,384,128]{2,1,0:T(8,128)(2,1)S(1)}) custom-call(s32[8,128]{1,0:T(8,128)S(1)} %convert_element_type.41.table.table0, s32[8,128]{1,0:T(8,128)S(1)} %convert_element_type.43.table1, ...), custom_call_target="tpu_custom_call", output_to_operand_aliasing={{2}: (4, {})} | custom-call | flops 1000000000 | bytes 8000000 | tf_op jit(solution)/shard_map/main_step/pallas_call | solution.py:203
  101.2 3.3 %collective-permute-start.7 = (bf16[8,384,128]{2,1,0:T(8,128)(2,1)S(1)}, bf16[8,384,128]{2,1,0:T(8,128)(2,1)S(1)}, u32[]{:S(2)}, u32[]{:S(2)}) collective-permute-start(bf16[8,384,128]{2,1,0:T(8,128)(2,1)S(1)} %get-tuple-element.17), channel_id=1, source_target_pairs={{0,1},{1,0},{2,3},{3,2},{4,5},{5,4},{6,7},{7,6},{8,9},{9,8},{10,11... | collective-permute-start | bytes 2359304 | tf_op jit(solution)/shard_map/ppermute | solution.py:273
  104.5 1.9 %rest_step.1 = bf16[8,384,128]{2,1,0:T(8,128)(2,1)S(1)} custom-call(s32[8,128]{1,0:T(8,128)S(1)} %convert_element_type.41.table.table0, bf16[12288,128]{1,0:T(8,128)(2,1)S(1)} %get-tuple-element.15.x, bf16[384,128]{1,0:T(8,128)(2,1)S(1)} %get-tuple-element.16.grad_t), custom_call_target="tpu_custom_call" | custom-call | flops 1000000000 | bytes 4000000 | tf_op jit(solution)/shard_map/rest_step/pallas_call | solution.py:222
  106.5 0.0 collective-permute-done.7
  106.5 1.1 add_convert_fusion
  107.6 7.2 %all-to-all-start.1 = ((bf16[8,384,128]{2,1,0:T(8,128)(2,1)}), bf16[8,384,128]{2,1,0:T(8,128)(2,1)S(1)}, u32[]{:S(2)}, u32[]{:S(2)}) async-start(bf16[8,384,128]{2,1,0:T(8,128)(2,1)} %add_convert_fusion), calls=%async_computation.1 | async-start | bytes 1572864 | tf_op jit(solution)/shard_map/all_to_all | solution.py:276
  114.8 23.6 %all-to-all-done.1 = bf16[8,384,128]{2,1,0:T(8,128)(2,1)S(1)} async-done(((bf16[8,384,128]{2,1,0:T(8,128)(2,1)}), bf16[8,384,128]{2,1,0:T(8,128)(2,1)S(1)}, u32[]{:S(2)}, u32[]{:S(2)}) %all-to-all-start.1) | async-done | bytes 786464 | tf_op jit(solution)/shard_map/all_to_all | solution.py:276
  138.3 0.1 convert_reduce_fusion
  138.4 0.1 reshape.231
  138.5 0.2 copy.13
  138.7 0.2 reshape.232
  138.9 0.7 select_convert_fusion
  (7 shorter events, 0.1 us)
Async XLA Ops:
  2.7 9.6 %copy-start.1 = (bf16[128,192]{0,1:T(8,128)(2,1)S(1)}, bf16[128,192]{0,1:T(8,128)(2,1)}, u32[]{:S(2)}) copy-start(bf16[128,192]{0,1:T(8,128)(2,1)} %param.5) | copy-start | bytes 147460
  4.6 48.5 %all-to-all-start = ((bf16[8,400,128]{2,1,0:T(8,128)(2,1)}), bf16[8,400,128]{2,1,0:T(8,128)(2,1)S(1)}, u32[]{:S(2)}, u32[]{:S(2)}) async-start(bf16[8,400,128]{2,1,0:T(8,128)(2,1)} %broadcast_in_dim.34), calls=%async_computation | async-start | bytes 1638400 | tf_op jit(solution)/shard_map/all_to_all | solution.py:253
  53.1 38.7 %collective-permute-start = (bf16[8,400,128]{2,1,0:T(8,128)(2,1)S(1)}, bf16[8,400,128]{2,1,0:T(8,128)(2,1)S(1)}, u32[]{:S(2)}, u32[]{:S(2)}) collective-permute-start(bf16[8,400,128]{2,1,0:T(8,128)(2,1)S(1)} %all-to-all-done.w), channel_id=1, source_target_pairs={{0,1},{1,0},{2,3},{3,2},{4,5},{5,4},{6,7},{7,6},{8,9},{9,8},{10,11... | collective-permute-start | bytes 2457608 | tf_op jit(solution)/shard_map/ppermute | solution.py:265
  62.9 12.9 %collective-permute-start.1 = (bf16[1536,128]{1,0:T(8,128)(2,1)}, bf16[1536,128]{1,0:T(8,128)(2,1)}, u32[]{:S(2)}, u32[]{:S(2)}) collective-permute-start(bf16[1536,128]{1,0:T(8,128)(2,1)} %bitcast.9), channel_id=1, source_target_pairs={{0,16},{16,0},{32,48},{48,32},{1,17},{17,1},{33,49},{49,33},{2,18}... | collective-permute-start | bytes 1179656 | tf_op jit(solution)/shard_map/ppermute | solution.py:259
  65.9 14.1 %collective-permute-start.4 = (bf16[1536,128]{1,0:T(8,128)(2,1)}, bf16[1536,128]{1,0:T(8,128)(2,1)}, u32[]{:S(2)}, u32[]{:S(2)}) collective-permute-start(bf16[1536,128]{1,0:T(8,128)(2,1)} %bitcast.10), channel_id=1, source_target_pairs={{0,48},{16,32},{32,16},{48,0},{1,49},{17,33},{33,17},{49,1},{2,50}... | collective-permute-start | bytes 1179656 | tf_op jit(solution)/shard_map/ppermute | solution.py:260
  69.6 18.5 %collective-permute-start.3 = (bf16[1536,128]{1,0:T(8,128)(2,1)}, bf16[1536,128]{1,0:T(8,128)(2,1)}, u32[]{:S(2)}, u32[]{:S(2)}) collective-permute-start(bf16[1536,128]{1,0:T(8,128)(2,1)} %bitcast.9), channel_id=1, source_target_pairs={{0,48},{16,32},{32,16},{48,0},{1,49},{17,33},{33,17},{49,1},{2,50}... | collective-permute-start | bytes 1179656 | tf_op jit(solution)/shard_map/ppermute | solution.py:262
  72.4 15.7 %collective-permute-start.2 = (bf16[1536,128]{1,0:T(8,128)(2,1)}, bf16[1536,128]{1,0:T(8,128)(2,1)}, u32[]{:S(2)}, u32[]{:S(2)}) collective-permute-start(bf16[1536,128]{1,0:T(8,128)(2,1)} %bitcast.10), channel_id=1, source_target_pairs={{0,16},{16,0},{32,48},{48,32},{1,17},{17,1},{33,49},{49,33},{2,18}... | collective-permute-start | bytes 1179656 | tf_op jit(solution)/shard_map/ppermute | solution.py:261
  75.7 20.7 %collective-permute-start.5 = (bf16[1536,128]{1,0:T(8,128)(2,1)}, bf16[1536,128]{1,0:T(8,128)(2,1)S(1)}, u32[]{:S(2)}, u32[]{:S(2)}) collective-permute-start(bf16[1536,128]{1,0:T(8,128)(2,1)} %collective-permute-done.1.x1a), channel_id=1, source_target_pairs={{0,48},{16,32},{32,16},{48,0},{1,49},{17,33},{33,17},{49,1},{2,50}... | collective-permute-start | bytes 1179656 | tf_op jit(solution)/shard_map/ppermute | solution.py:263
  80.0 16.4 %collective-permute-start.6 = (bf16[1536,128]{1,0:T(8,128)(2,1)}, bf16[1536,128]{1,0:T(8,128)(2,1)S(1)}, u32[]{:S(2)}, u32[]{:S(2)}) collective-permute-start(bf16[1536,128]{1,0:T(8,128)(2,1)} %collective-permute-done.4.x3b), channel_id=1, source_target_pairs={{0,16},{16,0},{32,48},{48,32},{1,17},{17,1},{33,49},{49,33},{2,18}... | collective-permute-start | bytes 1179656 | tf_op jit(solution)/shard_map/ppermute | solution.py:264
  88.1 8.3 %copy-start = (bf16[128,384]{1,0:T(8,128)(2,1)S(1)}, bf16[128,384]{1,0:T(8,128)(2,1)}, u32[]{:S(2)}) copy-start(bf16[128,384]{1,0:T(8,128)(2,1)} %up.1) | copy-start | bytes 294916
  101.2 5.3 %collective-permute-start.7 = (bf16[8,384,128]{2,1,0:T(8,128)(2,1)S(1)}, bf16[8,384,128]{2,1,0:T(8,128)(2,1)S(1)}, u32[]{:S(2)}, u32[]{:S(2)}) collective-permute-start(bf16[8,384,128]{2,1,0:T(8,128)(2,1)S(1)} %get-tuple-element.17), channel_id=1, source_target_pairs={{0,1},{1,0},{2,3},{3,2},{4,5},{5,4},{6,7},{7,6},{8,9},{9,8},{10,11... | collective-permute-start | bytes 2359304 | tf_op jit(solution)/shard_map/ppermute | solution.py:273
  107.6 30.8 %all-to-all-start.1 = ((bf16[8,384,128]{2,1,0:T(8,128)(2,1)}), bf16[8,384,128]{2,1,0:T(8,128)(2,1)S(1)}, u32[]{:S(2)}, u32[]{:S(2)}) async-start(bf16[8,384,128]{2,1,0:T(8,128)(2,1)} %add_convert_fusion), calls=%async_computation.1 | async-start | bytes 1572864 | tf_op jit(solution)/shard_map/all_to_all | solution.py:276

commit v6 on v5

--- a/solution.py
+++ b/solution.py
@@ -19,7 +19,8 @@
 NZ, NX, NY = 16, 4, 8
 SHARD = 192
 COL_ROWS = NZ * SHARD
-CUT = COL_ROWS // 2
+CUT = 7 * SHARD
+REST = COL_ROWS - CUT
 X_ROWS = NX * COL_ROWS
 UNITS = COL_ROWS // TILE
 GROUP = 8
@@ -120,14 +121,14 @@
 
     def part(distance, start, size):
         column = here[0] ^ distance
-        return x.at[pl.ds(pl.multiple_of(column * COL_ROWS + start, CUT), size), :]
+        return x.at[pl.ds(pl.multiple_of(column * COL_ROWS + start, TILE), size), :]
 
     moves = [
         (x0, part(0, 0, COL_ROWS)),
         (x1a, part(1, 0, CUT)),
-        (x1b, part(1, CUT, CUT)),
+        (x1b, part(1, CUT, REST)),
         (x3a, part(3, 0, CUT)),
-        (x3b, part(3, CUT, CUT)),
+        (x3b, part(3, CUT, REST)),
         (w, tiles),
     ]
     copies = [pltpu.make_async_copy(a, b, sem.at[i]) for i, (a, b) in enumerate(moves)]
@@ -145,8 +146,8 @@
 ):
     base = (here[0] ^ 2) * COL_ROWS
     copies = [
-        pltpu.make_async_copy(x2a, x.at[pl.ds(pl.multiple_of(base, CUT), CUT), :], sem.at[0]),
-        pltpu.make_async_copy(x2b, x.at[pl.ds(pl.multiple_of(base + CUT, CUT), CUT), :], sem.at[1]),
+        pltpu.make_async_copy(x2a, x.at[pl.ds(pl.multiple_of(base, TILE), CUT), :], sem.at[0]),
+        pltpu.make_async_copy(x2b, x.at[pl.ds(pl.multiple_of(base + CUT, TILE), REST), :], sem.at[1]),
     ]
     for c in copies:
         c.start()
@@ -254,7 +255,8 @@
 
     x_mine = activations.T.reshape(1, SHARD // 16, 16, TOK)
     x0 = lax.all_gather(x_mine, "z", axis=0, tiled=True).reshape(COL_ROWS, TOK)
-    lower, upper = x0[:CUT], x0[CUT:]
+    lower = x0[:CUT]
+    upper = lax.optimization_barrier(x0)[CUT:]
     near, far = trade(1), trade(3)
     x1a = lax.ppermute(lower, "x", near)
     x3b = lax.ppermute(upper, "x", far)

time: 140 us -> 155 us (1.11)
  blocking collectives: 40.8 us -> 62 us
  waiting for transfers between devices: 35.7 us -> 29.7 us
    all_to_all x0 -> x1, blocking collectives: none -> 22.8 us  [body(): w_own = lax.all_to_all(wide, 'y', split_axis=0, concat_axis=0, tiled=True)]
    all_to_all x1 -> x0, starting transfers between devices: 7.64 us -> none  [body(): w_own = lax.all_to_all(wide, 'y', split_axis=0, concat_axis=0, tiled=True)]
    ppermute x1, starting transfers between devices: 3.31 us -> 10.1 us  [body(): arrived = lax.ppermute(theirs, 'core', SWAP)]
    all_to_all x1, starting transfers between devices: 7.18 us -> 3.55 us  [body(): parts = lax.all_to_all(both, 'y', split_axis=0, concat_axis=0, tiled=True)]
    ppermute x1, waiting for transfers between devices: 6.13 us -> 2.71 us  [body(): x3a = lax.ppermute(lower, 'x', far)]
    ppermute x1, starting transfers between devices: 8.71 us -> 12 us  [body(): w_other = lax.ppermute(w_own, 'core', SWAP)]
    ppermute x1, waiting for transfers between devices: 4.58 us -> 2.55 us  [body(): x2a = lax.ppermute(x1a, 'x', far)]
    all_gather x1, blocking collectives: 40.8 us -> 39.2 us  [body(): x0 = lax.all_gather(x_mine, 'z', axis=0, tiled=True).reshape(COL_ROWS, TOK)]
  transfers between devices with their start and end apart: 10 -> 9, of which waited for: 4 -> 4; matrix products, arithmetic and copies ran while one was open for 1% -> 1% of each run, Pallas kernels for 4% -> 4%
where the time goes in v6:
time: 155 us; the launch traced here: 154 us
  blocking collectives  62 us (40%)
  starting transfers between devices  43.7 us (28%)
  waiting for transfers between devices  29.7 us (19%)
  Pallas kernels  10.8 us (7%)
  local copies, waits for them, and re-layouts  3.53 us (2%)
  other arithmetic  2.86 us (2%)
  between operations  1.55 us (1%)
    all_gather x1, blocking collectives, body(): x0 = lax.all_gather(x_mine, 'z', axis=0, tiled=True).reshape(COL_ROWS, TOK)  39.2 us
    all_to_all x1, waiting for transfers between devices, body(): parts = lax.all_to_all(both, 'y', split_axis=0, concat_axis=0, tiled=True)  23.5 us
    all_to_all x1, blocking collectives, body(): w_own = lax.all_to_all(wide, 'y', split_axis=0, concat_axis=0, tiled=True)  22.8 us
    ppermute x1, starting transfers between devices, body(): w_other = lax.ppermute(w_own, 'core', SWAP)  12 us
    ppermute x1, starting transfers between devices, body(): arrived = lax.ppermute(theirs, 'core', SWAP)  10.1 us
    pallas_call x1, Pallas kernels, main_step(): pl.pallas_call(main_kernel, out_shape=(jax.ShapeDtypeStruct((TOK, FF_LOC)...  5.32 us
    ppermute x1, starting transfers between devices, body(): x2a = lax.ppermute(x1a, 'x', far)  4.39 us
    ppermute x1, starting transfers between devices, body(): x3b = lax.ppermute(upper, 'x', far)  4.37 us
  transfers between devices with their start and end apart: 9, of which 4 were waited for; matrix products, arithmetic and copies ran while one was open for 1% of the time, Pallas kernels for 4%

profile of v6, /device:TPU:1, one launch (start us, length us, event | category | flops | bytes accessed | tf_op | source)
XLA Modules:
  0.0 154.2 jit_solution(15142069254915222598)
XLA Ops:
  1.3 1.1 reshape.225
  2.4 0.1 select_bitcast_fusion
  2.5 0.1 copy.12
  2.7 0.0 copy-start.1
  2.7 0.1 reshape.226
  2.8 0.7 fusion.1
  3.5 0.1 add_convert_fusion.1
  3.6 0.1 broadcast_in_dim.34
  3.7 22.8 %all_to_all.10.w = bf16[8,400,128]{2,1,0:T(8,128)(2,1)S(1)} all-to-all(bf16[8,400,128]{2,1,0:T(8,128)(2,1)S(1)} %broadcast_in_dim.34), channel_id=1, replica_groups=mesh['z'=16,'x'=4,'y'=8,'core'=2] {'y'}, dimensions={0} | all-to-all | bytes 1638400 | tf_op jit(solution)/shard_map/all_to_all | solution.py:254
  26.5 12.0 %collective-permute-start = (bf16[8,400,128]{2,1,0:T(8,128)(2,1)S(1)}, bf16[8,400,128]{2,1,0:T(8,128)(2,1)S(1)}, u32[]{:S(2)}, u32[]{:S(2)}) collective-permute-start(bf16[8,400,128]{2,1,0:T(8,128)(2,1)S(1)} %all_to_all.10.w), channel_id=1, source_target_pairs={{0,1},{1,0},{2,3},{3,2},{4,5},{5,4},{6,7},{7,6},{8,9},{9,8},{10,11... | collective-permute-start | bytes 2457608 | tf_op jit(solution)/shard_map/ppermute | solution.py:267
  38.6 0.0 copy-done.1
  38.6 39.2 %all_gather.3 = bf16[16,12,16,128]{3,2,1,0:T(8,128)(2,1)S(1)} all-gather(bf16[1,12,16,128]{3,2,1,0:T(8,128)(2,1)S(1)} %bitcast.32), channel_id=1, replica_groups=mesh['z'=16,'x'=4,'y'=8,'core'=2] {'z'}, dimensions={0}, use_global_device_ids=true | all-gather | bytes 835584 | tf_op jit(solution)/shard_map/all_gather | solution.py:257
  77.8 0.8 slice.23
  78.5 4.4 %collective-permute-start.4 = (bf16[1728,128]{1,0:T(8,128)(2,1)}, bf16[1728,128]{1,0:T(8,128)(2,1)S(1)}, u32[]{:S(2)}, u32[]{:S(2)}) collective-permute-start(bf16[1728,128]{1,0:T(8,128)(2,1)} %slice.23), channel_id=1, source_target_pairs={{0,48},{16,32},{32,16},{48,0},{1,49},{17,33},{33,17},{49,1},{2,50}... | collective-permute-start | bytes 1327112 | tf_op jit(solution)/shard_map/ppermute | solution.py:262
  82.9 0.8 slice.22
  83.7 1.9 %collective-permute-start.1 = (bf16[1344,128]{1,0:T(8,128)(2,1)}, bf16[1344,128]{1,0:T(8,128)(2,1)}, u32[]{:S(2)}, u32[]{:S(2)}) collective-permute-start(bf16[1344,128]{1,0:T(8,128)(2,1)} %bitcast.9), channel_id=1, source_target_pairs={{0,16},{16,0},{32,48},{48,32},{1,17},{17,1},{33,49},{49,33},{2,18}... | collective-permute-start | bytes 1032200 | tf_op jit(solution)/shard_map/ppermute | solution.py:261
  85.6 3.4 %collective-permute-start.2 = (bf16[1728,128]{1,0:T(8,128)(2,1)}, bf16[1728,128]{1,0:T(8,128)(2,1)}, u32[]{:S(2)}, u32[]{:S(2)}) collective-permute-start(bf16[1728,128]{1,0:T(8,128)(2,1)} %slice.23), channel_id=1, source_target_pairs={{0,16},{16,0},{32,48},{48,32},{1,17},{17,1},{33,49},{49,33},{2,18}... | collective-permute-start | bytes 1327112 | tf_op jit(solution)/shard_map/ppermute | solution.py:263
  89.0 2.1 %collective-permute-start.3 = (bf16[1344,128]{1,0:T(8,128)(2,1)}, bf16[1344,128]{1,0:T(8,128)(2,1)}, u32[]{:S(2)}, u32[]{:S(2)}) collective-permute-start(bf16[1344,128]{1,0:T(8,128)(2,1)} %bitcast.9), channel_id=1, source_target_pairs={{0,48},{16,32},{32,16},{48,0},{1,49},{17,33},{33,17},{49,1},{2,50}... | collective-permute-start | bytes 1032200 | tf_op jit(solution)/shard_map/ppermute | solution.py:264
  91.1 0.0 collective-permute-done.4.x3b
  91.1 1.9 %collective-permute-start.6 = (bf16[1728,128]{1,0:T(8,128)(2,1)S(1)}, bf16[1728,128]{1,0:T(8,128)(2,1)S(1)}, u32[]{:S(2)}, u32[]{:S(2)}) collective-permute-start(bf16[1728,128]{1,0:T(8,128)(2,1)S(1)} %collective-permute-done.4.x3b), channel_id=1, source_target_pairs={{0,16},{16,0},{32,48},{48,32},{1,17},{17,1},{33,49},{49,33},{2,18}... | collective-permute-start | bytes 1327112 | tf_op jit(solution)/shard_map/ppermute | solution.py:266
  93.0 0.0 collective-permute-done.1.x1a
  93.0 4.4 %collective-permute-start.5 = (bf16[1344,128]{1,0:T(8,128)(2,1)}, bf16[1344,128]{1,0:T(8,128)(2,1)}, u32[]{:S(2)}, u32[]{:S(2)}) collective-permute-start(bf16[1344,128]{1,0:T(8,128)(2,1)} %collective-permute-done.1.x1a), channel_id=1, source_target_pairs={{0,48},{16,32},{32,16},{48,0},{1,49},{17,33},{33,17},{49,1},{2,50}... | collective-permute-start | bytes 1032200 | tf_op jit(solution)/shard_map/ppermute | solution.py:265
  97.5 2.7 %collective-permute-done.3.x3a = bf16[1344,128]{1,0:T(8,128)(2,1)} collective-permute-done((bf16[1344,128]{1,0:T(8,128)(2,1)}, bf16[1344,128]{1,0:T(8,128)(2,1)}, u32[]{:S(2)}, u32[]{:S(2)}) %collective-permute-start.3) | collective-permute-done | bytes 344096 | tf_op jit(solution)/shard_map/ppermute | solution.py:264
  100.2 0.0 collective-permute-done.2.x1b
  100.2 0.0 copy-start
  100.2 3.6 %own_step.1 = (bf16[12288,128]{1,0:T(8,128)(2,1)S(1)}, bf16[8,400,128]{2,1,0:T(8,128)(2,1)S(1)}, f32[448,128]{1,0:T(8,128)S(1)}, s32[3,128]{1,0:T(4,128)S(1)}) custom-call(s32[8,128]{1,0:T(8,128)S(1)} %convert_element_type.41.table.table0, s32[1]{0:T(128)} %bitcast.5.here, bf16[3072,128]{1,0:T(8,128)(2,1)S(1)} %bitcast.30, ...), custom_call_target="tpu_custom_call" | custom-call | flops 500000000 | bytes 6000000 | tf_op jit(solution)/shard_map/own_step/pallas_call | solution.py:191
  103.7 0.0 collective-permute-done.tiles1
  103.8 2.6 %collective-permute-done.5.x2a = bf16[1344,128]{1,0:T(8,128)(2,1)} collective-permute-done((bf16[1344,128]{1,0:T(8,128)(2,1)}, bf16[1344,128]{1,0:T(8,128)(2,1)}, u32[]{:S(2)}, u32[]{:S(2)}) %collective-permute-start.5) | collective-permute-done | bytes 344096 | tf_op jit(solution)/shard_map/ppermute | solution.py:265
  106.3 0.9 collective-permute-done.6.x2b
  107.3 0.0 copy-done
  107.3 5.3 %main_step.1 = (bf16[128,384]{1,0:T(8,128)(2,1)}, bf16[384,128]{1,0:T(8,128)(2,1)S(1)}, bf16[12288,128]{1,0:T(8,128)(2,1)S(1)}, bf16[8,384,128]{2,1,0:T(8,128)(2,1)S(1)}) custom-call(s32[8,128]{1,0:T(8,128)S(1)} %convert_element_type.41.table.table0, s32[8,128]{1,0:T(8,128)S(1)} %convert_element_type.43.table1, ...), custom_call_target="tpu_custom_call", output_to_operand_aliasing={{2}: (4, {})} | custom-call | flops 1000000000 | bytes 8000000 | tf_op jit(solution)/shard_map/main_step/pallas_call | solution.py:204
  112.6 10.1 %collective-permute-start.7 = (bf16[8,384,128]{2,1,0:T(8,128)(2,1)S(1)}, bf16[8,384,128]{2,1,0:T(8,128)(2,1)S(1)}, u32[]{:S(2)}, u32[]{:S(2)}) collective-permute-start(bf16[8,384,128]{2,1,0:T(8,128)(2,1)S(1)} %get-tuple-element.17), channel_id=1, source_target_pairs={{0,1},{1,0},{2,3},{3,2},{4,5},{5,4},{6,7},{7,6},{8,9},{9,8},{10,11... | collective-permute-start | bytes 2359304 | tf_op jit(solution)/shard_map/ppermute | solution.py:275
  122.7 1.9 %rest_step.1 = bf16[8,384,128]{2,1,0:T(8,128)(2,1)S(1)} custom-call(s32[8,128]{1,0:T(8,128)S(1)} %convert_element_type.41.table.table0, bf16[12288,128]{1,0:T(8,128)(2,1)S(1)} %get-tuple-element.15.x, bf16[384,128]{1,0:T(8,128)(2,1)S(1)} %get-tuple-element.16.grad_t), custom_call_target="tpu_custom_call" | custom-call | flops 1000000000 | bytes 4000000 | tf_op jit(solution)/shard_map/rest_step/pallas_call | solution.py:223
  124.6 0.0 collective-permute-done.7
  124.6 1.1 add_convert_fusion
  125.7 3.5 %all-to-all-start.1 = ((bf16[8,384,128]{2,1,0:T(8,128)(2,1)}), bf16[8,384,128]{2,1,0:T(8,128)(2,1)S(1)}, u32[]{:S(2)}, u32[]{:S(2)}) async-start(bf16[8,384,128]{2,1,0:T(8,128)(2,1)} %add_convert_fusion), calls=%async_computation.1 | async-start | bytes 1572864 | tf_op jit(solution)/shard_map/all_to_all | solution.py:278
  129.3 23.5 %all-to-all-done.1 = bf16[8,384,128]{2,1,0:T(8,128)(2,1)S(1)} async-done(((bf16[8,384,128]{2,1,0:T(8,128)(2,1)}), bf16[8,384,128]{2,1,0:T(8,128)(2,1)S(1)}, u32[]{:S(2)}, u32[]{:S(2)}) %all-to-all-start.1) | async-done | bytes 786464 | tf_op jit(solution)/shard_map/all_to_all | solution.py:278
  152.8 0.1 convert_reduce_fusion
  152.9 0.1 reshape.230
  153.1 0.2 copy.13
  153.2 0.2 reshape.231
  153.4 0.7 select_convert_fusion
  (7 shorter events, 0.1 us)
Async XLA Ops:
  2.7 35.9 %copy-start.1 = (bf16[128,192]{0,1:T(8,128)(2,1)S(1)}, bf16[128,192]{0,1:T(8,128)(2,1)}, u32[]{:S(2)}) copy-start(bf16[128,192]{0,1:T(8,128)(2,1)} %param.5) | copy-start | bytes 147460
  26.5 77.2 %collective-permute-start = (bf16[8,400,128]{2,1,0:T(8,128)(2,1)S(1)}, bf16[8,400,128]{2,1,0:T(8,128)(2,1)S(1)}, u32[]{:S(2)}, u32[]{:S(2)}) collective-permute-start(bf16[8,400,128]{2,1,0:T(8,128)(2,1)S(1)} %all_to_all.10.w), channel_id=1, source_target_pairs={{0,1},{1,0},{2,3},{3,2},{4,5},{5,4},{6,7},{7,6},{8,9},{9,8},{10,11... | collective-permute-start | bytes 2457608 | tf_op jit(solution)/shard_map/ppermute | solution.py:267
  78.5 12.5 %collective-permute-start.4 = (bf16[1728,128]{1,0:T(8,128)(2,1)}, bf16[1728,128]{1,0:T(8,128)(2,1)S(1)}, u32[]{:S(2)}, u32[]{:S(2)}) collective-permute-start(bf16[1728,128]{1,0:T(8,128)(2,1)} %slice.23), channel_id=1, source_target_pairs={{0,48},{16,32},{32,16},{48,0},{1,49},{17,33},{33,17},{49,1},{2,50}... | collective-permute-start | bytes 1327112 | tf_op jit(solution)/shard_map/ppermute | solution.py:262
  83.7 9.3 %collective-permute-start.1 = (bf16[1344,128]{1,0:T(8,128)(2,1)}, bf16[1344,128]{1,0:T(8,128)(2,1)}, u32[]{:S(2)}, u32[]{:S(2)}) collective-permute-start(bf16[1344,128]{1,0:T(8,128)(2,1)} %bitcast.9), channel_id=1, source_target_pairs={{0,16},{16,0},{32,48},{48,32},{1,17},{17,1},{33,49},{49,33},{2,18}... | collective-permute-start | bytes 1032200 | tf_op jit(solution)/shard_map/ppermute | solution.py:261
  85.6 14.6 %collective-permute-start.2 = (bf16[1728,128]{1,0:T(8,128)(2,1)}, bf16[1728,128]{1,0:T(8,128)(2,1)}, u32[]{:S(2)}, u32[]{:S(2)}) collective-permute-start(bf16[1728,128]{1,0:T(8,128)(2,1)} %slice.23), channel_id=1, source_target_pairs={{0,16},{16,0},{32,48},{48,32},{1,17},{17,1},{33,49},{49,33},{2,18}... | collective-permute-start | bytes 1327112 | tf_op jit(solution)/shard_map/ppermute | solution.py:263
  89.0 11.2 %collective-permute-start.3 = (bf16[1344,128]{1,0:T(8,128)(2,1)}, bf16[1344,128]{1,0:T(8,128)(2,1)}, u32[]{:S(2)}, u32[]{:S(2)}) collective-permute-start(bf16[1344,128]{1,0:T(8,128)(2,1)} %bitcast.9), channel_id=1, source_target_pairs={{0,48},{16,32},{32,16},{48,0},{1,49},{17,33},{33,17},{49,1},{2,50}... | collective-permute-start | bytes 1032200 | tf_op jit(solution)/shard_map/ppermute | solution.py:264
  91.1 16.2 %collective-permute-start.6 = (bf16[1728,128]{1,0:T(8,128)(2,1)S(1)}, bf16[1728,128]{1,0:T(8,128)(2,1)S(1)}, u32[]{:S(2)}, u32[]{:S(2)}) collective-permute-start(bf16[1728,128]{1,0:T(8,128)(2,1)S(1)} %collective-permute-done.4.x3b), channel_id=1, source_target_pairs={{0,16},{16,0},{32,48},{48,32},{1,17},{17,1},{33,49},{49,33},{2,18}... | collective-permute-start | bytes 1327112 | tf_op jit(solution)/shard_map/ppermute | solution.py:266
  93.0 13.3 %collective-permute-start.5 = (bf16[1344,128]{1,0:T(8,128)(2,1)}, bf16[1344,128]{1,0:T(8,128)(2,1)}, u32[]{:S(2)}, u32[]{:S(2)}) collective-permute-start(bf16[1344,128]{1,0:T(8,128)(2,1)} %collective-permute-done.1.x1a), channel_id=1, source_target_pairs={{0,48},{16,32},{32,16},{48,0},{1,49},{17,33},{33,17},{49,1},{2,50}... | collective-permute-start | bytes 1032200 | tf_op jit(solution)/shard_map/ppermute | solution.py:265
  100.2 7.1 %copy-start = (bf16[128,384]{1,0:T(8,128)(2,1)S(1)}, bf16[128,384]{1,0:T(8,128)(2,1)}, u32[]{:S(2)}) copy-start(bf16[128,384]{1,0:T(8,128)(2,1)} %up.1) | copy-start | bytes 294916
  112.6 12.0 %collective-permute-start.7 = (bf16[8,384,128]{2,1,0:T(8,128)(2,1)S(1)}, bf16[8,384,128]{2,1,0:T(8,128)(2,1)S(1)}, u32[]{:S(2)}, u32[]{:S(2)}) collective-permute-start(bf16[8,384,128]{2,1,0:T(8,128)(2,1)S(1)} %get-tuple-element.17), channel_id=1, source_target_pairs={{0,1},{1,0},{2,3},{3,2},{4,5},{5,4},{6,7},{7,6},{8,9},{9,8},{10,11... | collective-permute-start | bytes 2359304 | tf_op jit(solution)/shard_map/ppermute | solution.py:275
  125.7 27.1 %all-to-all-start.1 = ((bf16[8,384,128]{2,1,0:T(8,128)(2,1)}), bf16[8,384,128]{2,1,0:T(8,128)(2,1)S(1)}, u32[]{:S(2)}, u32[]{:S(2)}) async-start(bf16[8,384,128]{2,1,0:T(8,128)(2,1)} %add_convert_fusion), calls=%async_computation.1 | async-start | bytes 1572864 | tf_op jit(solution)/shard_map/all_to_all | solution.py:278
